TPU v7x, 32 devices: a whole 2x2x4 slice. The times are simulated.
32 devices in a mesh: col: 4 (over y, x), dev: 4 (over z), ao: 2 (over core).
Axes of the slice: x: 2, y: 2, z: 4, core: 2. Of those that a mesh axis runs over, the one named last changes fastest.
Arguments:
- raw_ints: bfloat16 [1024, 32, 512], P('dev', None, 'col'), may hold values from -1.078125 to 1.078125
- metric: bfloat16 [1024, 1024], P('dev'), may hold values from -0.1875 to 0.1875
- amplitudes: bfloat16 [512, 512, 2048], P('col', 'dev', 'ao'), may hold values from -0.017944336 to 0.017944336
- pair_list: int32 [2, 2048], P(None, 'ao'), may hold values from 0 to 63
- occ_energy: float32 [64], replicated, may hold values from -2 to -0.3
- vir_energy: float32 [512], replicated, may hold values from 0.2 to 3
- window_ids: int32 [32], replicated, may hold values from 0 to 511, as said below
Outputs:
- residual: float32 [1024, 2048], P(('col', 'dev'), 'ao')
Inputs may be any that keep to these rules, and one draw needn't show every extreme that they name: `window_ids`: distinct virtual orbitals; 0 and 511 are always among them.
All inputs are finite; a program needn't handle non-finite values.
Results may differ from a plain program's by a relative error of at most 0.0041.
Values may be sent and summed in bfloat16 or wider, within the bound.
No kernel may reach another device: no remote copies, remote signals or barrier semaphores. Data moves between devices by JAX's collectives and lax.ppermute only.
A program may use at most 192 MiB of HBM per device.

v0:
```python
import functools

import jax
import jax.numpy as jnp
from jax import lax
from jax.experimental import pallas as pl
from jax.experimental.pallas import tpu as pltpu
from jax.sharding import PartitionSpec as P


def select_energy(positions, table):
    labels = jnp.arange(table.shape[0], dtype=jnp.int32)
    return jnp.sum(jnp.where(positions[:, None] == labels[None, :], table[None, :], 0.0), axis=1)


def general_plan(raw_ints, metric, amplitudes, pair_list, occ_energy, vir_energy, window_ids):
    full_width = raw_ints.shape[1]
    portion = full_width // lax.axis_size("ao")
    own_rows = lax.dynamic_slice_in_dim(raw_ints, lax.axis_index("ao") * portion, portion, 1)
    local_aux = metric.shape[0]
    rows_used = own_rows.shape[1]
    c_block = own_rows.shape[2]
    raw_block = lax.all_gather(own_rows, "dev", axis=0, tiled=True)
    row_count = raw_block.shape[0]
    transformed = jnp.dot(
        metric,
        raw_block.reshape(row_count, rows_used * c_block),
        preferred_element_type=jnp.float32,
    )
    transformed = transformed.astype(jnp.bfloat16).reshape(local_aux, rows_used, c_block)
    spread = lax.all_gather(transformed, "col", axis=2, tiled=True)
    right_factor = lax.all_to_all(spread, "dev", split_axis=2, concat_axis=0, tiled=True)
    d_block = right_factor.shape[2]
    contract = (((0,), (0,)), ((), ()))
    left_factor = lax.all_gather(transformed, "dev", axis=0, tiled=True)
    right_factor = lax.all_gather(right_factor, "ao", axis=1, tiled=True)
    all_aux = left_factor.shape[0]
    own_ladder = lax.dot_general(
        left_factor.reshape(all_aux, rows_used * c_block),
        right_factor.reshape(all_aux, full_width * d_block),
        contract,
        preferred_element_type=jnp.float32,
    )
    ladder_flat = lax.all_gather(own_ladder.astype(jnp.bfloat16), "ao", axis=0, tiled=True)
    ladder = ladder_flat.reshape(full_width, c_block, full_width, d_block)
    ladder = jnp.transpose(ladder, (0, 2, 1, 3)).reshape(full_width * full_width, c_block * d_block)
    partial_value = jnp.dot(
        ladder,
        amplitudes.reshape(c_block * d_block, amplitudes.shape[2]),
        preferred_element_type=jnp.float32,
    )
    summed = lax.psum_scatter(partial_value, ("col", "dev"), scatter_dimension=0, tiled=True)
    row_total = summed.shape[0]
    global_rows = lax.axis_index(("col", "dev")) * row_total + jnp.arange(
        row_total, dtype=jnp.int32
    )
    window_energy = select_energy(window_ids, vir_energy)
    energy_first = select_energy(global_rows // full_width, window_energy)
    energy_second = select_energy(global_rows % full_width, window_energy)
    energy_i = select_energy(pair_list[0], occ_energy)
    energy_j = select_energy(pair_list[1], occ_energy)
    denominator = (energy_i + energy_j)[None, :] - (energy_first + energy_second)[:, None]
    return summed / denominator


VMEM = 62 * 1024 * 1024


def on_ring(piece, axis):
    count = lax.axis_size(axis)
    pairs = [(place, (place + 1) % count) for place in range(count)]
    return lax.ppermute(piece, axis, pairs)


def flip(piece, axis, bit):
    pairs = [(place, place ^ 1 << bit) for place in range(lax.axis_size(axis))]
    return lax.ppermute(piece, axis, pairs)


def bits_of(count):
    return count.bit_length() - 1


def metric_kernel(devs, place_ref, *refs):
    whole_ref, turned_ref = refs[-2:]
    pieces = refs[:-2]
    count = len(pieces) // 2
    rows, aux = pieces[0].shape
    core, dev = place_ref[0], place_ref[1]
    block = aux // devs
    for half in range(2):
        for at in range(count):
            row = pl.multiple_of(((core ^ half) * count + at) * rows, rows)
            for step in range(devs):
                column = pl.multiple_of(lax.rem(dev - step + devs, devs) * block, block)
                whole_ref[pl.ds(row, rows), step * block : (step + 1) * block] = pieces[
                    half * count + at
                ][:, pl.ds(column, block)]
    turned_ref[...] = whole_ref[...].T


def whole_metric(metric):
    cols, devs, cores = lax.axis_size("col"), lax.axis_size("dev"), lax.axis_size("ao")
    share = metric.shape[0] // (cols * cores)
    at = (lax.axis_index("col") * cores + lax.axis_index("ao")) * share
    shares = [lax.dynamic_slice_in_dim(metric, at, share, 0)]
    for step in range(1, devs):
        pairs = [(dev, (dev + step) % devs) for dev in range(devs)]
        shares.append(lax.ppermute(shares[0], "dev", pairs))
    rows = [jnp.concatenate(shares, axis=0)]
    for turn in range(1, cols):
        rows.append(lax.ppermute(rows[0], "col", [(col, col ^ turn) for col in range(cols)]))
    rows += [flip(rows[turn], "ao", 0) for turn in range(cols)]
    place = jnp.stack([lax.axis_index("ao"), lax.axis_index("dev")]).astype(jnp.int32)
    shape = jax.ShapeDtypeStruct((metric.shape[0] * devs, metric.shape[1]), metric.dtype)
    return pl.pallas_call(
        functools.partial(metric_kernel, devs),
        in_specs=[pl.BlockSpec(memory_space=pltpu.SMEM)]
        + [pl.BlockSpec(memory_space=pltpu.VMEM)] * len(rows),
        out_specs=[pl.BlockSpec(memory_space=pltpu.VMEM)] * 2,
        out_shape=[shape, jax.ShapeDtypeStruct(shape.shape[::-1], metric.dtype)],
        compiler_params=pltpu.CompilerParams(vmem_limit_bytes=VMEM),
    )(place, *rows)


def left_kernel(metric_ref, *refs):
    rows = jnp.concatenate([ref[...] for ref in refs[:-1]], axis=2)
    count, width, depth = rows.shape
    product = jnp.dot(
        rows.reshape(count * width, depth), metric_ref[...], preferred_element_type=jnp.float32
    )
    refs[-1][...] = product.astype(jnp.bfloat16).reshape(count, width, product.shape[1])


def fit_left(metric_turned, pieces):
    c_block, width, depth = pieces[0].shape
    step = 32
    aux = metric_turned.shape[1]
    piece_spec = pl.BlockSpec((step, width, depth), lambda i: (i, 0, 0))
    return pl.pallas_call(
        left_kernel,
        grid=(c_block // step,),
        in_specs=[pl.BlockSpec(metric_turned.shape, lambda i: (0, 0))] + [piece_spec] * len(pieces),
        out_specs=pl.BlockSpec((step, width, aux), lambda i: (i, 0, 0)),
        out_shape=jax.ShapeDtypeStruct((c_block, width, aux), jnp.bfloat16),
        compiler_params=pltpu.CompilerParams(vmem_limit_bytes=VMEM),
        cost_estimate=pl.CostEstimate(
            flops=2 * metric_turned.size * c_block * width,
            bytes_accessed=2 * (metric_turned.size + 2 * c_block * width * aux),
            transcendentals=0,
        ),
    )(metric_turned, *pieces)


def fit_kernel(arrived_ref, metric_ref, *refs):
    out_ref, held, sems = refs[-3:]
    pieces = refs[:-3]
    count = len(pieces) // 2
    width = held.shape[2]
    step = pl.program_id(0)

    def fetch(at, slot):
        for piece in range(count):
            for came in range(2):

                @pl.when(arrived_ref[piece % 2] == came)
                def _(piece=piece, came=came):
                    pltpu.make_async_copy(
                        pieces[2 * piece + came].at[pl.ds(at * width, width)],
                        held.at[slot, piece],
                        sems.at[slot, piece],
                    ).start()

    @pl.when(step == 0)
    def _():
        fetch(0, 0)

    slot = lax.rem(step, 2)

    @pl.when(step + 1 < pl.num_programs(0))
    def _():
        fetch(step + 1, 1 - slot)

    for piece in range(count):
        pltpu.make_async_copy(
            pieces[2 * piece].at[pl.ds(step * width, width)],
            held.at[slot, piece],
            sems.at[slot, piece],
        ).wait()
    columns = [
        jnp.concatenate([held[slot, piece, b] for piece in range(count)], axis=0)
        for b in range(width)
    ]
    out_ref[...] = jnp.dot(
        metric_ref[...], jnp.concatenate(columns, axis=1), preferred_element_type=jnp.float32
    ).astype(out_ref.dtype)


def fit_right(arrived, metric_all, flat):
    width, depth, d_block = flat[0].shape
    step = 4
    aux = metric_all.shape[0]
    count = len(flat) // 2
    part = count * depth
    return pl.pallas_call(
        fit_kernel,
        grid=(width // step,),
        in_specs=[
            pl.BlockSpec(memory_space=pltpu.SMEM),
            pl.BlockSpec((aux, part), lambda i: (0, 0)),
        ]
        + [pl.BlockSpec(memory_space=pl.ANY)] * len(flat),
        out_specs=pl.BlockSpec((aux, step * d_block), lambda i: (0, i)),
        out_shape=jax.ShapeDtypeStruct((aux, width * d_block), jnp.float32),
        scratch_shapes=[
            pltpu.VMEM((2, count, step, depth, d_block), jnp.bfloat16),
            pltpu.SemaphoreType.DMA((2, count)),
        ],
        compiler_params=pltpu.CompilerParams(vmem_limit_bytes=24 * 1024 * 1024),
        cost_estimate=pl.CostEstimate(
            flops=2 * aux * part * width * d_block,
            bytes_accessed=2 * (aux * part + count * flat[0].size + 2 * aux * width * d_block),
            transcendentals=0,
        ),
    )(arrived, metric_all, *flat)


def ladder_kernel(
    arrived_ref, metric_ref, own_ref, other_ref, early_ref, *refs
):
    ladder_ref, right_ref, sums_ref, held, sum_sems, sems = refs[-6:]
    pieces = refs[:-6]
    count = len(pieces) // 2
    c_count, width, depth = own_ref.shape
    d_block = ladder_ref.shape[1] // c_count
    right_rows = right_ref.shape[1] // d_block
    parts, _, columns = sums_ref.shape

    @pl.when(pl.program_id(0) == 0)
    def _():
        for piece in range(count):
            for came in range(2):

                @pl.when(arrived_ref[piece % 2] == came)
                def _(piece=piece, came=came):
                    pltpu.make_async_copy(
                        pieces[2 * piece + came], held.at[piece], sems.at[piece]
                    ).start()

        fetched = [
            pltpu.make_async_copy(
                early_ref.at[:, pl.ds(part * columns, columns)], sums_ref.at[part], sum_sems.at[part]
            )
            for part in range(parts)
        ]
        for copy in fetched:
            copy.start()
        for piece in range(count):
            pltpu.make_async_copy(pieces[2 * piece], held.at[piece], sems.at[piece]).wait()
        many = columns // d_block
        for part in range(parts):
            fetched[part].wait()
            late = [
                jnp.concatenate([held[piece, part * many + b] for piece in range(count)], axis=0)
                for b in range(many)
            ]
            product = jnp.dot(
                metric_ref[...], jnp.concatenate(late, axis=1), preferred_element_type=jnp.float32
            )
            right_ref[:, part * columns : (part + 1) * columns] = (
                product + sums_ref[part]
            ).astype(right_ref.dtype)

    for half, ref in enumerate((own_ref, other_ref)):
        product = jnp.dot(
            ref[...].reshape(c_count * width, depth),
            right_ref[...],
            preferred_element_type=jnp.float32,
        ).astype(jnp.bfloat16)
        for c in range(c_count):
            for b in range(right_rows):
                row = (b * 2 + half) * width
                ladder_ref[row : row + width, c * d_block : (c + 1) * d_block] = product[
                    c * width : (c + 1) * width, b * d_block : (b + 1) * d_block
                ]


def ladder_of(arrived, metric_all, own_left, other_left, early, flat):
    c_block, width, depth = own_left.shape
    right_rows, rows_late, d_block = flat[0].shape
    step, parts = 16, 4
    count = len(flat) // 2
    part = count * rows_late
    aux, columns = early.shape
    left_spec = pl.BlockSpec((step, width, depth), lambda i: (i, 0, 0))
    rows = right_rows * 2 * width
    return pl.pallas_call(
        ladder_kernel,
        grid=(c_block // step,),
        in_specs=[
            pl.BlockSpec(memory_space=pltpu.SMEM),
            pl.BlockSpec((aux, part), lambda i: (0, metric_all.shape[1] // part - 1)),
            left_spec,
            left_spec,
        ]
        + [pl.BlockSpec(memory_space=pl.ANY)] * (1 + len(flat)),
        out_specs=pl.BlockSpec((rows, step * d_block), lambda i: (0, i)),
        out_shape=jax.ShapeDtypeStruct((rows, c_block * d_block), jnp.bfloat16),
        scratch_shapes=[
            pltpu.VMEM((aux, columns), jnp.bfloat16),
            pltpu.VMEM((parts, aux, columns // parts), jnp.float32),
            pltpu.VMEM((count, right_rows, rows_late, d_block), jnp.bfloat16),
            pltpu.SemaphoreType.DMA((parts,)),
            pltpu.SemaphoreType.DMA((count,)),
        ],
        compiler_params=pltpu.CompilerParams(vmem_limit_bytes=30 * 1024 * 1024),
        cost_estimate=pl.CostEstimate(
            flops=4 * c_block * width * depth * columns + 2 * aux * part * columns,
            bytes_accessed=2 * (2 * own_left.size + 2 * early.size + rows * c_block * d_block),
            transcendentals=0,
        ),
    )(arrived, metric_all, own_left, other_left, early, *flat)


def contract_kernel(ladder_ref, amplitudes_ref, out_ref, total_ref):
    @pl.when(pl.program_id(0) == 0)
    def _():
        total_ref[...] = jnp.zeros_like(total_ref)

    product = jnp.dot(ladder_ref[...], amplitudes_ref[...], preferred_element_type=jnp.float32)
    tiles, _, lanes = total_ref.shape
    for tile in range(tiles):
        total_ref[tile] += product[:, tile * lanes : (tile + 1) * lanes]

    @pl.when(pl.program_id(0) == pl.num_programs(0) - 1)
    def _():
        owners, rows, _ = out_ref.shape
        for owner in range(owners):
            for tile in range(tiles):
                out_ref[owner, :, tile * lanes : (tile + 1) * lanes] = total_ref[
                    tile, pl.ds(owner, rows, stride=owners), :
                ].astype(out_ref.dtype)


def contract(ladder, amplitudes, owners):
    rows, depth = ladder.shape
    columns = amplitudes.shape[1]
    step = 4096
    return pl.pallas_call(
        contract_kernel,
        grid=(depth // step,),
        in_specs=[
            pl.BlockSpec((rows, step), lambda i: (0, i)),
            pl.BlockSpec((step, columns), lambda i: (i, 0)),
        ],
        out_specs=pl.BlockSpec((owners, rows // owners, columns), lambda i: (0, 0, 0)),
        out_shape=jax.ShapeDtypeStruct((owners, rows // owners, columns), jnp.bfloat16),
        scratch_shapes=[pltpu.VMEM((columns // 128, rows, 128), jnp.float32)],
        compiler_params=pltpu.CompilerParams(vmem_limit_bytes=VMEM),
        cost_estimate=pl.CostEstimate(
            flops=2 * rows * depth * columns,
            bytes_accessed=2 * (rows * depth + depth * columns + rows * columns),
            transcendentals=0,
        ),
    )(ladder, amplitudes)


def spread(partial):
    return lax.all_to_all(partial, ("col", "dev"), split_axis=0, concat_axis=0, tiled=True)


def total_of(parts):
    return jnp.sum(parts.astype(jnp.float32), axis=0)


def plan_on_device(raw_ints, metric, amplitudes, pair_list, occ_energy, vir_energy, window_ids):
    aux, full_width, c_block = raw_ints.shape
    cols, devs = lax.axis_size("col"), lax.axis_size("dev")
    core = lax.axis_index("ao")
    width = full_width // 2
    own = lax.dynamic_index_in_dim(raw_ints.reshape(aux, width, 2, c_block), core, 2, keepdims=False)
    own = jnp.transpose(own, (1, 0, 2))
    half = aux // 2
    here = list(lax.optimization_barrier((own[:, :half], own[:, half:])))
    metric_all, metric_turned = whole_metric(metric)
    away = lax.axis_index("col") ^ lax.axis_index("dev")
    bits = bits_of(cols)
    bit_set = [(away >> bit) & 1 for bit in range(bits)]
    came = [flag == 1 for flag in bit_set]
    *came, away = lax.optimization_barrier((*came, away))
    arrived = jnp.stack([bit_set[(h + bits - 1) % bits] for h in range(2)]).astype(jnp.int32)
    pieces, left_pieces = [], []
    for s in range(devs):
        for h in range(2):
            left_pieces.append(jnp.transpose(here[h], (2, 0, 1)))
        if s < devs - 1:
            ahead = [on_ring(here[h], "dev") for h in range(2)]
        else:
            own_left = fit_left(metric_turned, left_pieces)
        held = here
        for hop in range(bits):
            if hop:
                held = [
                    jnp.where(came[(h + hop - 1) % bits], last[h], held[h]) for h in range(2)
                ]
                held = list(lax.optimization_barrier(tuple(held)))
            last = [flip(held[h], "col", (h + hop) % bits) for h in range(2)]
        pieces += [held[0], last[0], held[1], last[1]]
        here = ahead
    other_left = flip(own_left, "ao", 0)
    early = fit_right(arrived, metric_all, pieces[:-4])
    own_ladder = ladder_of(arrived, metric_all, own_left, other_left, early, pieces[-4:])
    other_ladder = flip(own_ladder, "ao", 0)
    flat_amplitudes = amplitudes.reshape(c_block * amplitudes.shape[1], amplitudes.shape[2])
    own_partial = contract(own_ladder, flat_amplitudes, width)
    own_parts = spread(own_partial)
    other_partial = contract(other_ladder, flat_amplitudes, width)
    other_parts = spread(other_partial)
    sums = [
        total_of(parts).reshape(width, 2, parts.shape[2]) for parts in (own_parts, other_parts)
    ]
    (own_same, own_cross), (other_same, other_cross) = [(s[:, 0], s[:, 1]) for s in sums]
    first = core == 0

    def by_core(zero, one):
        return jnp.where(first, zero, one)

    even_a = jnp.stack([by_core(own_same, other_same), by_core(other_cross, own_cross)], axis=1)
    odd_a = jnp.stack([by_core(own_cross, other_cross), by_core(other_same, own_same)], axis=1)
    summed = jnp.stack([even_a, odd_a]).reshape(2 * full_width, amplitudes.shape[2])
    row_total = summed.shape[0]
    global_rows = lax.axis_index(("col", "dev")) * row_total + jnp.arange(
        row_total, dtype=jnp.int32
    )
    window_energy = select_energy(window_ids, vir_energy)
    energy_first = select_energy(global_rows // full_width, window_energy)
    energy_second = select_energy(global_rows % full_width, window_energy)
    energy_i = select_energy(pair_list[0], occ_energy)
    energy_j = select_energy(pair_list[1], occ_energy)
    denominator = (energy_i + energy_j)[None, :] - (energy_first + energy_second)[:, None]
    return summed / denominator


def on_device(raw_ints, *rest):
    cols, devs, cores = lax.axis_size("col"), lax.axis_size("dev"), lax.axis_size("ao")
    _, full_width, c_block = raw_ints.shape
    paired = cols == devs and cores == 2 and full_width == 2 * cols * devs
    if paired and cols & (cols - 1) == 0 and c_block % 128 == 0:
        return plan_on_device(raw_ints, *rest)
    return general_plan(raw_ints, *rest)


def solution(mesh):
    in_specs = (
        P("dev", None, "col"),
        P("dev", None),
        P("col", "dev", "ao"),
        P(None, "ao"),
        P(),
        P(),
        P(),
    )
    out_specs = P(("col", "dev"), "ao")
    return jax.shard_map(
        on_device, mesh=mesh, in_specs=in_specs, out_specs=out_specs, check_vma=False
    )
```

profile of v0, /device:TPU:0, one launch (start us, length us, event | category | flops | bytes accessed | tf_op | source)
XLA Modules:
  0.0 319.2 jit_solution(4638693860077402530)
XLA Ops:
  0.0 3.8 %constant_dynamic-slice_fusion = bf16[256,16,1,128]{3,2,1,0:T(2,128)(2,1)S(1)} fusion(bf16[256,16,2,128]{3,2,1,0:T(2,128)(2,1)} %bitcast.28, s32[]{:T(128)S(6)} %select_n.109), kind=kLoop, calls=%fused_computation.38 | loop fusion | bytes 2097156 | tf_op jit(solution)/shard_map/jit(dynamic_index_in_dim)/dynamic_slice | solution.py:381
  4.6 3.1 collective-permute-start.11
  7.7 1.6 collective-permute-start.10
  9.3 13.3 %collective-permute-done.11 = bf16[16,128,128]{2,1,0:T(8,128)(2,1)} collective-permute-done((bf16[16,128,128]{2,1,0:T(8,128)(2,1)S(1)}, bf16[16,128,128]{2,1,0:T(8,128)(2,1)}, u32[]{:S(2)}, u32[]{:S(2)}) %collective-permute-start.11) | collective-permute-done | bytes 524320 | tf_op jit(solution)/shard_map/ppermute | solution.py:72
  22.6 11.2 %collective-permute-done.10 = bf16[16,128,128]{2,1,0:T(8,128)(2,1)} collective-permute-done((bf16[16,128,128]{2,1,0:T(8,128)(2,1)S(1)}, bf16[16,128,128]{2,1,0:T(8,128)(2,1)}, u32[]{:S(2)}, u32[]{:S(2)}) %collective-permute-start.10) | collective-permute-done | bytes 524320 | tf_op jit(solution)/shard_map/ppermute | solution.py:72
  33.8 1.6 collective-permute-start
  35.5 2.8 collective-permute-start.1
  39.4 18.3 %collective-permute-done = bf16[32,1024]{1,0:T(8,128)(2,1)S(1)} collective-permute-done((bf16[32,1024]{1,0:T(8,128)(2,1)S(1)}, bf16[32,1024]{1,0:T(8,128)(2,1)S(1)}, u32[]{:S(2)}, u32[]{:S(2)}) %collective-permute-start) | collective-permute-done | bytes 65568 | tf_op jit(solution)/shard_map/ppermute | solution.py:109
  57.7 2.0 collective-permute-done.1
  59.7 1.6 collective-permute-start.3
  61.3 1.5 collective-permute-start.4
  63.3 5.7 %collective-permute-done.3.refs_1_ = bf16[128,1024]{1,0:T(8,128)(2,1)S(1)} collective-permute-done((bf16[128,1024]{1,0:T(8,128)(2,1)S(1)}, bf16[128,1024]{1,0:T(8,128)(2,1)S(1)}, u32[]{:S(2)}, u32[]{:S(2)}) %collective-permute-start.3) | collective-permute-done | bytes 262176 | tf_op jit(solution)/shard_map/ppermute | solution.py:112
  69.0 1.9 collective-permute-start.14
  71.0 3.8 %collective-permute-done.4.refs_2_ = bf16[128,1024]{1,0:T(8,128)(2,1)S(1)} collective-permute-done((bf16[128,1024]{1,0:T(8,128)(2,1)S(1)}, bf16[128,1024]{1,0:T(8,128)(2,1)S(1)}, u32[]{:S(2)}, u32[]{:S(2)}) %collective-permute-start.4) | collective-permute-done | bytes 262176 | tf_op jit(solution)/shard_map/ppermute | solution.py:112
  78.4 2.2 copy.20.refs_2_
  80.6 2.2 copy.21.refs_3_
  83.6 3.9 %shard_map.73 = (bf16[1024,1024]{1,0:T(8,128)(2,1)}, bf16[1024,1024]{1,0:T(8,128)(2,1)}) custom-call(s32[2]{0:T(128)} %pad_add_fusion.1.place_ref, bf16[128,1024]{1,0:T(8,128)(2,1)} %copy-done.6, bf16[128,1024]{1,0:T(8,128)(2,1)} %copy-done.7, bf16[128,1024]{1,0:T(8,128)(2,1)} %copy-done.8, bf16[128,1024]{1,0:T(8,128)(2,1)} %copy-done.9, ...), custom_call_target="tpu_custom_call" | custom-call | tf_op jit(solution)/shard_map/pallas_call | solution.py:116
  87.5 2.2 copy.22.refs_4_
  89.7 2.2 copy.23.refs_5_
  93.1 3.6 %collective-permute-done.15 = bf16[16,128,128]{2,1,0:T(8,128)(2,1)} collective-permute-done((bf16[16,128,128]{2,1,0:T(8,128)(2,1)}, bf16[16,128,128]{2,1,0:T(8,128)(2,1)}, u32[]{:S(2)}, u32[]{:S(2)}) %collective-permute-start.15) | collective-permute-done | bytes 524320 | tf_op jit(solution)/shard_map/ppermute | solution.py:72
  96.7 2.2 copy.25.refs_7_
  98.9 8.7 %shard_map.74.own_ref = bf16[128,16,1024]{2,1,0:T(8,128)(2,1)} custom-call(bf16[1024,1024]{1,0:T(8,128)(2,1)} %get-tuple-element.20.metric_ref, bf16[128,16,128]{2,1,0:T(8,128)(2,1)} %copy.18.refs_0_, bf16[128,16,128]{2,1,0:T(8,128)(2,1)} %copy.19.refs_1_, bf16[128,16,128]{2,1,0:T(8,128)(2,1)} %copy.20.refs_2_, bf16[128,16,128]{2,1,0:T(8,128)(2,1)} %copy.21.refs_3_, ...), custom_call_target="tpu_custom_call" | custom-call | flops 4294967296 | bytes 10485760 | tf_op jit(solution)/shard_map/pallas_call | solution.py:140
  107.7 1.6 collective-permute-start.18
  109.3 1.5 collective-permute-start.17
  111.8 10.7 %collective-permute-done.18 = bf16[16,128,128]{2,1,0:T(8,128)(2,1)S(1)} collective-permute-done((bf16[16,128,128]{2,1,0:T(8,128)(2,1)S(1)}, bf16[16,128,128]{2,1,0:T(8,128)(2,1)S(1)}, u32[]{:S(2)}, u32[]{:S(2)}) %collective-permute-start.18) | collective-permute-done | bytes 524320 | tf_op jit(solution)/shard_map/ppermute | solution.py:77
  122.6 1.4 collective-permute-done.17
  124.7 1.5 collective-permute-start.26
  126.2 7.6 %collective-permute-done.22 = bf16[16,128,128]{2,1,0:T(8,128)(2,1)S(1)} collective-permute-done((bf16[16,128,128]{2,1,0:T(8,128)(2,1)}, bf16[16,128,128]{2,1,0:T(8,128)(2,1)S(1)}, u32[]{:S(2)}, u32[]{:S(2)}) %collective-permute-start.22) | collective-permute-done | bytes 524320 | tf_op jit(solution)/shard_map/ppermute | solution.py:77
  133.8 1.5 collective-permute-start.25
  138.1 17.6 %collective-permute-done.26 = bf16[16,128,128]{2,1,0:T(8,128)(2,1)S(1)} collective-permute-done((bf16[16,128,128]{2,1,0:T(8,128)(2,1)}, bf16[16,128,128]{2,1,0:T(8,128)(2,1)S(1)}, u32[]{:S(2)}, u32[]{:S(2)}) %collective-permute-start.26) | collective-permute-done | bytes 524320 | tf_op jit(solution)/shard_map/ppermute | solution.py:77
  155.7 1.5 collective-permute-start.30
  157.2 1.5 collective-permute-start.29
  161.3 9.4 %collective-permute-done.30 = bf16[16,128,128]{2,1,0:T(8,128)(2,1)S(1)} collective-permute-done((bf16[16,128,128]{2,1,0:T(8,128)(2,1)}, bf16[16,128,128]{2,1,0:T(8,128)(2,1)S(1)}, u32[]{:S(2)}, u32[]{:S(2)}) %collective-permute-start.30) | collective-permute-done | bytes 524320 | tf_op jit(solution)/shard_map/ppermute | solution.py:77
  170.7 1.5 collective-permute-start.27
  172.2 1.5 collective-permute-start.28
  174.9 7.1 %collective-permute-done.23.refs_5_ = bf16[16,128,128]{2,1,0:T(8,128)(2,1)S(1)} collective-permute-done((bf16[16,128,128]{2,1,0:T(8,128)(2,1)S(1)}, bf16[16,128,128]{2,1,0:T(8,128)(2,1)S(1)}, u32[]{:S(2)}, u32[]{:S(2)}) %collective-permute-start.23) | collective-permute-done | bytes 524320 | tf_op jit(solution)/shard_map/ppermute | solution.py:77
  181.9 1.5 collective-permute-start.31
  183.5 1.5 collective-permute-start.32
  185.0 8.1 %collective-permute-done.27.refs_9_ = bf16[16,128,128]{2,1,0:T(8,128)(2,1)S(1)} collective-permute-done((bf16[16,128,128]{2,1,0:T(8,128)(2,1)S(1)}, bf16[16,128,128]{2,1,0:T(8,128)(2,1)S(1)}, u32[]{:S(2)}, u32[]{:S(2)}) %collective-permute-start.27) | collective-permute-done | bytes 524320 | tf_op jit(solution)/shard_map/ppermute | solution.py:77
  193.2 1.3 collective-permute-done.28.refs_11_
  194.5 9.7 %shard_map.75.early_ref = f32[1024,2048]{1,0:T(8,128)S(1)} custom-call(s32[2]{0:T(128)S(1)} %pad_add_fusion.arrived_ref, bf16[1024,1024]{1,0:T(8,128)(2,1)S(1)} %copy-done.2, bf16[16,128,128]{2,1,0:T(8,128)(2,1)S(1)} %broadcast_select_fusion.7.refs_0_, bf16[16,128,128]{2,1,0:T(8,128)(2,1)S(1)} %collective-permute-done.19.refs_1_, ...), custom_call_target="tpu_custom_call" | custom-call | flops 3221225472 | bytes 13107200 | tf_op jit(solution)/shard_map/pallas_call | solution.py:205
  204.2 24.8 %shard_map.76.ladder_ref = bf16[512,16384]{1,0:T(8,128)(2,1)} custom-call(s32[2]{0:T(128)S(1)} %pad_add_fusion.arrived_ref, bf16[1024,1024]{1,0:T(8,128)(2,1)S(1)} %copy-done.2, bf16[128,16,1024]{2,1,0:T(8,128)(2,1)S(1)} %copy-done.3, bf16[128,16,1024]{2,1,0:T(8,128)(2,1)} %collective-permute-done.16.other_ref, f32[1024,2048]{1,0:T(8,128)S(1)} %shard_map.75.early_ref, ...), custom_call_target="tpu_custom_call" | custom-call | flops 18253611008 | bytes 33554432 | tf_op jit(solution)/shard_map/pallas_call | solution.py:297
  229.1 24.8 %shard_map.77 = bf16[16,32,1024]{2,1,0:T(8,128)(2,1)} custom-call(bf16[512,16384]{1,0:T(8,128)(2,1)} %shard_map.76.ladder_ref, bf16[16384,1024]{1,0:T(8,128)(2,1)} %bitcast.32), custom_call_target="tpu_custom_call" | custom-call | flops 17179869184 | bytes 51380224 | tf_op jit(solution)/shard_map/pallas_call | solution.py:349
  253.9 3.9 %all-to-all-start = ((bf16[16,32,1024]{2,1,0:T(8,128)(2,1)}), bf16[16,32,1024]{2,1,0:T(8,128)(2,1)S(1)}, u32[]{:S(2)}, u32[]{:S(2)}) async-start(bf16[16,32,1024]{2,1,0:T(8,128)(2,1)} %shard_map.77), calls=%async_computation | async-start | bytes 2097152 | tf_op jit(solution)/shard_map/all_to_all | solution.py:369
  257.8 24.9 %shard_map.78 = bf16[16,32,1024]{2,1,0:T(8,128)(2,1)} custom-call(bf16[512,16384]{1,0:T(8,128)(2,1)} %collective-permute-done.33.ladder_ref, bf16[16384,1024]{1,0:T(8,128)(2,1)} %bitcast.33), custom_call_target="tpu_custom_call" | custom-call | flops 17179869184 | bytes 51380224 | tf_op jit(solution)/shard_map/pallas_call | solution.py:349
  282.7 3.3 %all-to-all-done = bf16[16,32,1024]{2,1,0:T(8,128)(2,1)S(1)} async-done(((bf16[16,32,1024]{2,1,0:T(8,128)(2,1)}), bf16[16,32,1024]{2,1,0:T(8,128)(2,1)S(1)}, u32[]{:S(2)}, u32[]{:S(2)}) %all-to-all-start) | async-done | bytes 1048608 | tf_op jit(solution)/shard_map/all_to_all | solution.py:369
  285.9 3.7 %all-to-all-start.1 = ((bf16[16,32,1024]{2,1,0:T(8,128)(2,1)}), bf16[16,32,1024]{2,1,0:T(8,128)(2,1)S(1)}, u32[]{:S(2)}, u32[]{:S(2)}) async-start(bf16[16,32,1024]{2,1,0:T(8,128)(2,1)} %shard_map.78), calls=%async_computation.1 | async-start | bytes 2097152 | tf_op jit(solution)/shard_map/all_to_all | solution.py:369
  290.4 26.9 %all-to-all-done.1 = bf16[16,32,1024]{2,1,0:T(8,128)(2,1)S(1)} async-done(((bf16[16,32,1024]{2,1,0:T(8,128)(2,1)}), bf16[16,32,1024]{2,1,0:T(8,128)(2,1)S(1)}, u32[]{:S(2)}, u32[]{:S(2)}) %all-to-all-start.1) | async-done | bytes 1048608 | tf_op jit(solution)/shard_map/all_to_all | solution.py:369
  (101 shorter events, 18.9 us)
Async XLA Ops:
  0.0 33.8 %copy-start = (bf16[256,1024]{1,0:T(8,128)(2,1)S(1)}, bf16[256,1024]{1,0:T(8,128)(2,1)}, u32[]{:S(2)}) copy-start(bf16[256,1024]{1,0:T(8,128)(2,1)} %param.8) | copy-start | bytes 1572868
  4.6 18.0 %collective-permute-start.11 = (bf16[16,128,128]{2,1,0:T(8,128)(2,1)S(1)}, bf16[16,128,128]{2,1,0:T(8,128)(2,1)}, u32[]{:S(2)}, u32[]{:S(2)}) collective-permute-start(bf16[16,128,128]{2,1,0:T(8,128)(2,1)S(1)} %get-tuple-element.22), channel_id=1, source_target_pairs={{0,2},{2,4},{4,6},{6,0},{1,3},{3,5},{5,7},{7,1},{8,10},{10,12},{12... | collective-permute-start | bytes 1572872 | tf_op jit(solution)/shard_map/ppermute | solution.py:72
  7.7 26.1 %collective-permute-start.10 = (bf16[16,128,128]{2,1,0:T(8,128)(2,1)S(1)}, bf16[16,128,128]{2,1,0:T(8,128)(2,1)}, u32[]{:S(2)}, u32[]{:S(2)}) collective-permute-start(bf16[16,128,128]{2,1,0:T(8,128)(2,1)S(1)} %get-tuple-element.21), channel_id=1, source_target_pairs={{0,2},{2,4},{4,6},{6,0},{1,3},{3,5},{5,7},{7,1},{8,10},{10,12},{12... | collective-permute-start | bytes 1572872 | tf_op jit(solution)/shard_map/ppermute | solution.py:72
  22.6 48.3 %collective-permute-start.13 = (bf16[16,128,128]{2,1,0:T(8,128)(2,1)}, bf16[16,128,128]{2,1,0:T(8,128)(2,1)}, u32[]{:S(2)}, u32[]{:S(2)}) collective-permute-start(bf16[16,128,128]{2,1,0:T(8,128)(2,1)} %collective-permute-done.11), channel_id=1, source_target_pairs={{0,2},{2,4},{4,6},{6,0},{1,3},{3,5},{5,7},{7,1},{8,10},{10,12},{12... | collective-permute-start | bytes 1572872 | tf_op jit(solution)/shard_map/ppermute | solution.py:72
  33.8 35.2 %collective-permute-start.12 = (bf16[16,128,128]{2,1,0:T(8,128)(2,1)}, bf16[16,128,128]{2,1,0:T(8,128)(2,1)}, u32[]{:S(2)}, u32[]{:S(2)}) collective-permute-start(bf16[16,128,128]{2,1,0:T(8,128)(2,1)} %collective-permute-done.10), channel_id=1, source_target_pairs={{0,2},{2,4},{4,6},{6,0},{1,3},{3,5},{5,7},{7,1},{8,10},{10,12},{12... | collective-permute-start | bytes 1572872 | tf_op jit(solution)/shard_map/ppermute | solution.py:72
  33.8 23.8 %collective-permute-start = (bf16[32,1024]{1,0:T(8,128)(2,1)S(1)}, bf16[32,1024]{1,0:T(8,128)(2,1)S(1)}, u32[]{:S(2)}, u32[]{:S(2)}) collective-permute-start(bf16[32,1024]{1,0:T(8,128)(2,1)S(1)} %constant_dynamic-slice_fusion.1), channel_id=1, source_target_pairs={{0,2},{2,4},{4,6},{6,0},{1,3},{3,5},{5,7},{7,1},{8,10},{10,12},{12... | collective-permute-start | bytes 196616 | tf_op jit(solution)/shard_map/ppermute | solution.py:109
  35.5 24.2 %collective-permute-start.1 = (bf16[32,1024]{1,0:T(8,128)(2,1)S(1)}, bf16[32,1024]{1,0:T(8,128)(2,1)S(1)}, u32[]{:S(2)}, u32[]{:S(2)}) collective-permute-start(bf16[32,1024]{1,0:T(8,128)(2,1)S(1)} %constant_dynamic-slice_fusion.1), channel_id=1, source_target_pairs={{0,4},{2,6},{4,0},{6,2},{1,5},{3,7},{5,1},{7,3},{8,12},{10,14},{12... | collective-permute-start | bytes 196616 | tf_op jit(solution)/shard_map/ppermute | solution.py:109
  38.3 21.4 %collective-permute-start.2 = (bf16[32,1024]{1,0:T(8,128)(2,1)S(1)}, bf16[32,1024]{1,0:T(8,128)(2,1)S(1)}, u32[]{:S(2)}, u32[]{:S(2)}) collective-permute-start(bf16[32,1024]{1,0:T(8,128)(2,1)S(1)} %constant_dynamic-slice_fusion.1), channel_id=1, source_target_pairs={{0,6},{2,0},{4,2},{6,4},{1,7},{3,1},{5,3},{7,5},{8,14},{10,8},{12,... | collective-permute-start | bytes 196616 | tf_op jit(solution)/shard_map/ppermute | solution.py:109
  59.7 23.1 %copy-start.6 = (bf16[128,1024]{1,0:T(8,128)(2,1)}, bf16[128,1024]{1,0:T(8,128)(2,1)S(1)}, u32[]{:S(2)}) copy-start(bf16[128,1024]{1,0:T(8,128)(2,1)S(1)} %pad_maximum_fusion.refs_0_) | copy-start | bytes 786436
  59.7 9.2 %collective-permute-start.3 = (bf16[128,1024]{1,0:T(8,128)(2,1)S(1)}, bf16[128,1024]{1,0:T(8,128)(2,1)S(1)}, u32[]{:S(2)}, u32[]{:S(2)}) collective-permute-start(bf16[128,1024]{1,0:T(8,128)(2,1)S(1)} %pad_maximum_fusion.refs_0_), channel_id=1, source_target_pairs={{0,8},{8,0},{16,24},{24,16},{1,9},{9,1},{17,25},{25,17},{2,10},{10... | collective-permute-start | bytes 786440 | tf_op jit(solution)/shard_map/ppermute | solution.py:112
  61.3 13.5 %collective-permute-start.4 = (bf16[128,1024]{1,0:T(8,128)(2,1)S(1)}, bf16[128,1024]{1,0:T(8,128)(2,1)S(1)}, u32[]{:S(2)}, u32[]{:S(2)}) collective-permute-start(bf16[128,1024]{1,0:T(8,128)(2,1)S(1)} %pad_maximum_fusion.refs_0_), channel_id=1, source_target_pairs={{0,16},{8,24},{16,0},{24,8},{1,17},{9,25},{17,1},{25,9},{2,18},{10... | collective-permute-start | bytes 786440 | tf_op jit(solution)/shard_map/ppermute | solution.py:112
  62.8 12.0 %collective-permute-start.5 = (bf16[128,1024]{1,0:T(8,128)(2,1)S(1)}, bf16[128,1024]{1,0:T(8,128)(2,1)S(1)}, u32[]{:S(2)}, u32[]{:S(2)}) collective-permute-start(bf16[128,1024]{1,0:T(8,128)(2,1)S(1)} %pad_maximum_fusion.refs_0_), channel_id=1, source_target_pairs={{0,24},{8,16},{16,8},{24,0},{1,25},{9,17},{17,9},{25,1},{2,26},{10... | collective-permute-start | bytes 786440 | tf_op jit(solution)/shard_map/ppermute | solution.py:112
  69.0 13.9 %copy-start.7 = (bf16[128,1024]{1,0:T(8,128)(2,1)}, bf16[128,1024]{1,0:T(8,128)(2,1)S(1)}, u32[]{:S(2)}) copy-start(bf16[128,1024]{1,0:T(8,128)(2,1)S(1)} %collective-permute-done.3.refs_1_) | copy-start | bytes 786436
  69.0 6.3 %collective-permute-start.6 = (bf16[128,1024]{1,0:T(8,128)(2,1)S(1)}, bf16[128,1024]{1,0:T(8,128)(2,1)S(1)}, u32[]{:S(2)}, u32[]{:S(2)}) collective-permute-start(bf16[128,1024]{1,0:T(8,128)(2,1)S(1)} %pad_maximum_fusion.refs_0_), channel_id=1, source_target_pairs={{0,1},{1,0},{2,3},{3,2},{4,5},{5,4},{6,7},{7,6},{8,9},{9,8},{10,11... | collective-permute-start | bytes 786440 | tf_op jit(solution)/shard_map/ppermute | solution.py:77
  69.0 22.9 %collective-permute-start.14 = (bf16[16,128,128]{2,1,0:T(8,128)(2,1)}, bf16[16,128,128]{2,1,0:T(8,128)(2,1)S(1)}, u32[]{:S(2)}, u32[]{:S(2)}) collective-permute-start(bf16[16,128,128]{2,1,0:T(8,128)(2,1)} %collective-permute-done.12), channel_id=1, source_target_pairs={{0,2},{2,4},{4,6},{6,0},{1,3},{3,5},{5,7},{7,1},{8,10},{10,12},{12... | collective-permute-start | bytes 1572872 | tf_op jit(solution)/shard_map/ppermute | solution.py:72
  70.9 25.8 %collective-permute-start.15 = (bf16[16,128,128]{2,1,0:T(8,128)(2,1)}, bf16[16,128,128]{2,1,0:T(8,128)(2,1)}, u32[]{:S(2)}, u32[]{:S(2)}) collective-permute-start(bf16[16,128,128]{2,1,0:T(8,128)(2,1)} %collective-permute-done.13), channel_id=1, source_target_pairs={{0,2},{2,4},{4,6},{6,0},{1,3},{3,5},{5,7},{7,1},{8,10},{10,12},{12... | collective-permute-start | bytes 1572872 | tf_op jit(solution)/shard_map/ppermute | solution.py:72
  74.8 8.1 %copy-start.8 = (bf16[128,1024]{1,0:T(8,128)(2,1)}, bf16[128,1024]{1,0:T(8,128)(2,1)S(1)}, u32[]{:S(2)}) copy-start(bf16[128,1024]{1,0:T(8,128)(2,1)S(1)} %collective-permute-done.4.refs_2_) | copy-start | bytes 786436
  74.8 8.1 %collective-permute-start.7 = (bf16[128,1024]{1,0:T(8,128)(2,1)S(1)}, bf16[128,1024]{1,0:T(8,128)(2,1)S(1)}, u32[]{:S(2)}, u32[]{:S(2)}) collective-permute-start(bf16[128,1024]{1,0:T(8,128)(2,1)S(1)} %collective-permute-done.3.refs_1_), channel_id=1, source_target_pairs={{0,1},{1,0},{2,3},{3,2},{4,5},{5,4},{6,7},{7,6},{8,9},{9,8},{10,11... | collective-permute-start | bytes 786440 | tf_op jit(solution)/shard_map/ppermute | solution.py:77
  74.8 8.1 %copy-start.9 = (bf16[128,1024]{1,0:T(8,128)(2,1)}, bf16[128,1024]{1,0:T(8,128)(2,1)S(1)}, u32[]{:S(2)}) copy-start(bf16[128,1024]{1,0:T(8,128)(2,1)S(1)} %collective-permute-done.5.refs_3_) | copy-start | bytes 786436
  74.8 8.1 %collective-permute-start.8 = (bf16[128,1024]{1,0:T(8,128)(2,1)S(1)}, bf16[128,1024]{1,0:T(8,128)(2,1)}, u32[]{:S(2)}, u32[]{:S(2)}) collective-permute-start(bf16[128,1024]{1,0:T(8,128)(2,1)S(1)} %collective-permute-done.4.refs_2_), channel_id=1, source_target_pairs={{0,1},{1,0},{2,3},{3,2},{4,5},{5,4},{6,7},{7,6},{8,9},{9,8},{10,11... | collective-permute-start | bytes 786440 | tf_op jit(solution)/shard_map/ppermute | solution.py:77
  75.3 7.6 %copy-start.10 = (bf16[128,1024]{1,0:T(8,128)(2,1)}, bf16[128,1024]{1,0:T(8,128)(2,1)S(1)}, u32[]{:S(2)}) copy-start(bf16[128,1024]{1,0:T(8,128)(2,1)S(1)} %collective-permute-done.6.refs_4_) | copy-start | bytes 786436
  75.3 8.3 %collective-permute-start.9 = (bf16[128,1024]{1,0:T(8,128)(2,1)S(1)}, bf16[128,1024]{1,0:T(8,128)(2,1)}, u32[]{:S(2)}, u32[]{:S(2)}) collective-permute-start(bf16[128,1024]{1,0:T(8,128)(2,1)S(1)} %collective-permute-done.5.refs_3_), channel_id=1, source_target_pairs={{0,1},{1,0},{2,3},{3,2},{4,5},{5,4},{6,7},{7,6},{8,9},{9,8},{10,11... | collective-permute-start | bytes 786440 | tf_op jit(solution)/shard_map/ppermute | solution.py:77
  91.9 15.7 %copy-start.4 = (bf16[16,128,128]{2,1,0:T(8,128)(2,1)}, bf16[16,128,128]{2,1,0:T(8,128)(2,1)S(1)}, u32[]{:S(2)}) copy-start(bf16[16,128,128]{2,1,0:T(8,128)(2,1)S(1)} %collective-permute-done.14) | copy-start | bytes 1572868
  107.6 96.6 %collective-permute-start.16 = (bf16[128,16,1024]{2,1,0:T(8,128)(2,1)}, bf16[128,16,1024]{2,1,0:T(8,128)(2,1)}, u32[]{:S(2)}, u32[]{:S(2)}) collective-permute-start(bf16[128,16,1024]{2,1,0:T(8,128)(2,1)} %shard_map.74.own_ref), channel_id=1, source_target_pairs={{0,1},{1,0},{2,3},{3,2},{4,5},{5,4},{6,7},{7,6},{8,9},{9,8},{10,11... | collective-permute-start | bytes 12582920 | tf_op jit(solution)/shard_map/ppermute | solution.py:77
  107.7 14.9 %collective-permute-start.18 = (bf16[16,128,128]{2,1,0:T(8,128)(2,1)S(1)}, bf16[16,128,128]{2,1,0:T(8,128)(2,1)S(1)}, u32[]{:S(2)}, u32[]{:S(2)}) collective-permute-start(bf16[16,128,128]{2,1,0:T(8,128)(2,1)S(1)} %get-tuple-element.22), channel_id=1, source_target_pairs={{0,16},{8,24},{16,0},{24,8},{1,17},{9,25},{17,1},{25,9},{2,18},{10... | collective-permute-start | bytes 1572872 | tf_op jit(solution)/shard_map/ppermute | solution.py:77
  109.3 14.8 %collective-permute-start.17 = (bf16[16,128,128]{2,1,0:T(8,128)(2,1)S(1)}, bf16[16,128,128]{2,1,0:T(8,128)(2,1)S(1)}, u32[]{:S(2)}, u32[]{:S(2)}) collective-permute-start(bf16[16,128,128]{2,1,0:T(8,128)(2,1)S(1)} %get-tuple-element.21), channel_id=1, source_target_pairs={{0,8},{8,0},{16,24},{24,16},{1,9},{9,1},{17,25},{25,17},{2,10},{10... | collective-permute-start | bytes 1572872 | tf_op jit(solution)/shard_map/ppermute | solution.py:77
  110.7 23.0 %collective-permute-start.22 = (bf16[16,128,128]{2,1,0:T(8,128)(2,1)}, bf16[16,128,128]{2,1,0:T(8,128)(2,1)S(1)}, u32[]{:S(2)}, u32[]{:S(2)}) collective-permute-start(bf16[16,128,128]{2,1,0:T(8,128)(2,1)} %collective-permute-done.11), channel_id=1, source_target_pairs={{0,16},{8,24},{16,0},{24,8},{1,17},{9,25},{17,1},{25,9},{2,18},{10... | collective-permute-start | bytes 1572872 | tf_op jit(solution)/shard_map/ppermute | solution.py:77
  111.3 25.1 %collective-permute-start.21 = (bf16[16,128,128]{2,1,0:T(8,128)(2,1)}, bf16[16,128,128]{2,1,0:T(8,128)(2,1)S(1)}, u32[]{:S(2)}, u32[]{:S(2)}) collective-permute-start(bf16[16,128,128]{2,1,0:T(8,128)(2,1)} %collective-permute-done.10), channel_id=1, source_target_pairs={{0,8},{8,0},{16,24},{24,16},{1,9},{9,1},{17,25},{25,17},{2,10},{10... | collective-permute-start | bytes 1572872 | tf_op jit(solution)/shard_map/ppermute | solution.py:77
  122.6 34.6 %copy-start.5 = (bf16[16,128,128]{2,1,0:T(8,128)(2,1)S(1)}, bf16[16,128,128]{2,1,0:T(8,128)(2,1)}, u32[]{:S(2)}) copy-start(bf16[16,128,128]{2,1,0:T(8,128)(2,1)} %copy-done.4) | copy-start | bytes 1572868
  124.1 37.0 %collective-permute-start.19 = (bf16[16,128,128]{2,1,0:T(8,128)(2,1)S(1)}, bf16[16,128,128]{2,1,0:T(8,128)(2,1)S(1)}, u32[]{:S(2)}, u32[]{:S(2)}) collective-permute-start(bf16[16,128,128]{2,1,0:T(8,128)(2,1)S(1)} %broadcast_select_fusion.7.refs_0_), channel_id=1, source_target_pairs={{0,16},{8,24},{16,0},{24,8},{1,17},{9,25},{17,1},{25,9},{2,18},{10... | collective-permute-start | bytes 1572872 | tf_op jit(solution)/shard_map/ppermute | solution.py:77
  124.7 31.0 %collective-permute-start.26 = (bf16[16,128,128]{2,1,0:T(8,128)(2,1)}, bf16[16,128,128]{2,1,0:T(8,128)(2,1)S(1)}, u32[]{:S(2)}, u32[]{:S(2)}) collective-permute-start(bf16[16,128,128]{2,1,0:T(8,128)(2,1)} %collective-permute-done.13), channel_id=1, source_target_pairs={{0,16},{8,24},{16,0},{24,8},{1,17},{9,25},{17,1},{25,9},{2,18},{10... | collective-permute-start | bytes 1572872 | tf_op jit(solution)/shard_map/ppermute | solution.py:77
  133.8 23.5 %collective-permute-start.25 = (bf16[16,128,128]{2,1,0:T(8,128)(2,1)}, bf16[16,128,128]{2,1,0:T(8,128)(2,1)S(1)}, u32[]{:S(2)}, u32[]{:S(2)}) collective-permute-start(bf16[16,128,128]{2,1,0:T(8,128)(2,1)} %collective-permute-done.12), channel_id=1, source_target_pairs={{0,8},{8,0},{16,24},{24,16},{1,9},{9,1},{17,25},{25,17},{2,10},{10... | collective-permute-start | bytes 1572872 | tf_op jit(solution)/shard_map/ppermute | solution.py:77
  136.4 24.8 %collective-permute-start.20 = (bf16[16,128,128]{2,1,0:T(8,128)(2,1)S(1)}, bf16[16,128,128]{2,1,0:T(8,128)(2,1)S(1)}, u32[]{:S(2)}, u32[]{:S(2)}) collective-permute-start(bf16[16,128,128]{2,1,0:T(8,128)(2,1)S(1)} %broadcast_select_fusion.3.refs_2_), channel_id=1, source_target_pairs={{0,8},{8,0},{16,24},{24,16},{1,9},{9,1},{17,25},{25,17},{2,10},{10... | collective-permute-start | bytes 1572872 | tf_op jit(solution)/shard_map/ppermute | solution.py:77
  155.7 15.0 %collective-permute-start.30 = (bf16[16,128,128]{2,1,0:T(8,128)(2,1)}, bf16[16,128,128]{2,1,0:T(8,128)(2,1)S(1)}, u32[]{:S(2)}, u32[]{:S(2)}) collective-permute-start(bf16[16,128,128]{2,1,0:T(8,128)(2,1)} %collective-permute-done.15), channel_id=1, source_target_pairs={{0,16},{8,24},{16,0},{24,8},{1,17},{9,25},{17,1},{25,9},{2,18},{10... | collective-permute-start | bytes 1572872 | tf_op jit(solution)/shard_map/ppermute | solution.py:77
  157.2 15.0 %collective-permute-start.29 = (bf16[16,128,128]{2,1,0:T(8,128)(2,1)S(1)}, bf16[16,128,128]{2,1,0:T(8,128)(2,1)S(1)}, u32[]{:S(2)}, u32[]{:S(2)}) collective-permute-start(bf16[16,128,128]{2,1,0:T(8,128)(2,1)S(1)} %copy-done.5), channel_id=1, source_target_pairs={{0,8},{8,0},{16,24},{24,16},{1,9},{9,1},{17,25},{25,17},{2,10},{10... | collective-permute-start | bytes 1572872 | tf_op jit(solution)/shard_map/ppermute | solution.py:77
  159.8 34.7 %copy-start.2 = (bf16[1024,1024]{1,0:T(8,128)(2,1)S(1)}, bf16[1024,1024]{1,0:T(8,128)(2,1)}, u32[]{:S(2)}) copy-start(bf16[1024,1024]{1,0:T(8,128)(2,1)} %get-tuple-element.19.metric_ref) | copy-start | bytes 6291460
  161.1 20.8 %collective-permute-start.23 = (bf16[16,128,128]{2,1,0:T(8,128)(2,1)S(1)}, bf16[16,128,128]{2,1,0:T(8,128)(2,1)S(1)}, u32[]{:S(2)}, u32[]{:S(2)}) collective-permute-start(bf16[16,128,128]{2,1,0:T(8,128)(2,1)S(1)} %broadcast_select_fusion.6.refs_4_), channel_id=1, source_target_pairs={{0,16},{8,24},{16,0},{24,8},{1,17},{9,25},{17,1},{25,9},{2,18},{10... | collective-permute-start | bytes 1572872 | tf_op jit(solution)/shard_map/ppermute | solution.py:77
  161.2 22.3 %collective-permute-start.24 = (bf16[16,128,128]{2,1,0:T(8,128)(2,1)S(1)}, bf16[16,128,128]{2,1,0:T(8,128)(2,1)S(1)}, u32[]{:S(2)}, u32[]{:S(2)}) collective-permute-start(bf16[16,128,128]{2,1,0:T(8,128)(2,1)S(1)} %broadcast_select_fusion.2.refs_6_), channel_id=1, source_target_pairs={{0,8},{8,0},{16,24},{24,16},{1,9},{9,1},{17,25},{25,17},{2,10},{10... | collective-permute-start | bytes 1572872 | tf_op jit(solution)/shard_map/ppermute | solution.py:77
  170.7 22.5 %collective-permute-start.27 = (bf16[16,128,128]{2,1,0:T(8,128)(2,1)S(1)}, bf16[16,128,128]{2,1,0:T(8,128)(2,1)S(1)}, u32[]{:S(2)}, u32[]{:S(2)}) collective-permute-start(bf16[16,128,128]{2,1,0:T(8,128)(2,1)S(1)} %broadcast_select_fusion.5.refs_8_), channel_id=1, source_target_pairs={{0,16},{8,24},{16,0},{24,8},{1,17},{9,25},{17,1},{25,9},{2,18},{10... | collective-permute-start | bytes 1572872 | tf_op jit(solution)/shard_map/ppermute | solution.py:77
  172.2 22.3 %collective-permute-start.28 = (bf16[16,128,128]{2,1,0:T(8,128)(2,1)S(1)}, bf16[16,128,128]{2,1,0:T(8,128)(2,1)S(1)}, u32[]{:S(2)}, u32[]{:S(2)}) collective-permute-start(bf16[16,128,128]{2,1,0:T(8,128)(2,1)S(1)} %broadcast_select_fusion.1.refs_10_), channel_id=1, source_target_pairs={{0,8},{8,0},{16,24},{24,16},{1,9},{9,1},{17,25},{25,17},{2,10},{10... | collective-permute-start | bytes 1572872 | tf_op jit(solution)/shard_map/ppermute | solution.py:77
  181.9 22.2 %collective-permute-start.31 = (bf16[16,128,128]{2,1,0:T(8,128)(2,1)S(1)}, bf16[16,128,128]{2,1,0:T(8,128)(2,1)S(1)}, u32[]{:S(2)}, u32[]{:S(2)}) collective-permute-start(bf16[16,128,128]{2,1,0:T(8,128)(2,1)S(1)} %broadcast_select_fusion.4.refs_0_), channel_id=1, source_target_pairs={{0,16},{8,24},{16,0},{24,8},{1,17},{9,25},{17,1},{25,9},{2,18},{10... | collective-permute-start | bytes 1572872 | tf_op jit(solution)/shard_map/ppermute | solution.py:77
  183.5 20.7 %collective-permute-start.32 = (bf16[16,128,128]{2,1,0:T(8,128)(2,1)S(1)}, bf16[16,128,128]{2,1,0:T(8,128)(2,1)S(1)}, u32[]{:S(2)}, u32[]{:S(2)}) collective-permute-start(bf16[16,128,128]{2,1,0:T(8,128)(2,1)S(1)} %broadcast_select_fusion.refs_2_), channel_id=1, source_target_pairs={{0,8},{8,0},{16,24},{24,16},{1,9},{9,1},{17,25},{25,17},{2,10},{10... | collective-permute-start | bytes 1572872 | tf_op jit(solution)/shard_map/ppermute | solution.py:77
  194.5 9.7 %copy-start.3 = (bf16[128,16,1024]{2,1,0:T(8,128)(2,1)S(1)}, bf16[128,16,1024]{2,1,0:T(8,128)(2,1)}, u32[]{:S(2)}) copy-start(bf16[128,16,1024]{2,1,0:T(8,128)(2,1)} %shard_map.74.own_ref) | copy-start | bytes 12582916
  229.0 28.8 %collective-permute-start.33 = (bf16[512,16384]{1,0:T(8,128)(2,1)}, bf16[512,16384]{1,0:T(8,128)(2,1)}, u32[]{:S(2)}, u32[]{:S(2)}) collective-permute-start(bf16[512,16384]{1,0:T(8,128)(2,1)} %shard_map.76.ladder_ref), channel_id=1, source_target_pairs={{0,1},{1,0},{2,3},{3,2},{4,5},{5,4},{6,7},{7,6},{8,9},{9,8},{10,11... | collective-permute-start | bytes 50331656 | tf_op jit(solution)/shard_map/ppermute | solution.py:77
  253.9 32.0 %all-to-all-start = ((bf16[16,32,1024]{2,1,0:T(8,128)(2,1)}), bf16[16,32,1024]{2,1,0:T(8,128)(2,1)S(1)}, u32[]{:S(2)}, u32[]{:S(2)}) async-start(bf16[16,32,1024]{2,1,0:T(8,128)(2,1)} %shard_map.77), calls=%async_computation | async-start | bytes 2097152 | tf_op jit(solution)/shard_map/all_to_all | solution.py:369
  282.7 7.3 %copy-start.14 = (f32[64]{0:T(128)S(1)}, f32[64]{0:T(128)}, u32[]{:S(2)}) copy-start(f32[64]{0:T(128)} %param.11) | copy-start | bytes 772
  285.9 31.4 %all-to-all-start.1 = ((bf16[16,32,1024]{2,1,0:T(8,128)(2,1)}), bf16[16,32,1024]{2,1,0:T(8,128)(2,1)S(1)}, u32[]{:S(2)}, u32[]{:S(2)}) async-start(bf16[16,32,1024]{2,1,0:T(8,128)(2,1)} %shard_map.78), calls=%async_computation.1 | async-start | bytes 2097152 | tf_op jit(solution)/shard_map/all_to_all | solution.py:369
  290.3 28.8 %copy-start.1 = (bf16[256,1024]{1,0:T(8,128)(2,1)S(1)}, bf16[256,1024]{1,0:T(8,128)(2,1)}, u32[]{:S(2)}) copy-start(bf16[256,1024]{1,0:T(8,128)(2,1)} %param.8) | copy-start | bytes 1572868
  (4 other events, 21.9 us)
where the time goes:
time: 320 us; the launch traced here: 319 us
  waiting for transfers between devices  151 us (47%)
  Pallas kernels  96.7 us (30%)
  starting transfers between devices  41.5 us (13%)
  local copies, waits for them, and re-layouts  20.4 us (6%)
  other arithmetic  8.7 us (3%)
    ppermute x22, waiting for transfers between devices, flip(): return lax.ppermute(piece, axis, pairs)  63.4 us
    pallas_call x2, Pallas kernels, contract(): pl.pallas_call(contract_kernel, grid=(depth // step,), in_specs=[pl.Block...  49.7 us
    all_to_all x2, waiting for transfers between devices, spread(): lax.all_to_all(partial, ('col', 'dev'), split_axis=0, concat_axis=0, tile...  30.2 us
    ppermute x6, waiting for transfers between devices, on_ring(): return lax.ppermute(piece, axis, pairs)  28.1 us
    pallas_call x1, Pallas kernels, ladder_of(): pl.pallas_call(ladder_kernel, grid=(c_block // step,), in_specs=[pl.Block...  24.8 us
    ppermute x3, waiting for transfers between devices, whole_metric(): shares.append(lax.ppermute(shares[0], 'dev', pairs))  20.3 us
    ppermute x22, starting transfers between devices, flip(): return lax.ppermute(piece, axis, pairs)  18.2 us
    transpose x8, local copies, waits for them, and re-layouts, plan_on_device(): left_pieces.append(jnp.transpose(here[h], (2, 0, 1)))  14.8 us
  transfers between devices with their start and end apart: 36, of which 17 were waited for; matrix products, arithmetic and copies ran while one was open for 6% of the time, Pallas kernels for 20%

commit v1 on v0

--- a/solution.py
+++ b/solution.py
@@ -356,7 +356,7 @@
         out_specs=pl.BlockSpec((owners, rows // owners, columns), lambda i: (0, 0, 0)),
         out_shape=jax.ShapeDtypeStruct((owners, rows // owners, columns), jnp.bfloat16),
         scratch_shapes=[pltpu.VMEM((columns // 128, rows, 128), jnp.float32)],
-        compiler_params=pltpu.CompilerParams(vmem_limit_bytes=VMEM),
+        compiler_params=pltpu.CompilerParams(vmem_limit_bytes=40 * 1024 * 1024),
         cost_estimate=pl.CostEstimate(
             flops=2 * rows * depth * columns,
             bytes_accessed=2 * (rows * depth + depth * columns + rows * columns),
@@ -367,6 +367,13 @@
 
 def spread(partial):
     return lax.all_to_all(partial, ("col", "dev"), split_axis=0, concat_axis=0, tiled=True)
+
+
+def spread_twice(partial):
+    cols, devs = lax.axis_size("col"), lax.axis_size("dev")
+    plane = lax.all_to_all(partial, "col", split_axis=0, concat_axis=0, tiled=True)
+    plane = total_of(plane.reshape(cols, devs, *partial.shape[1:])).astype(partial.dtype)
+    return lax.all_to_all(plane, "dev", split_axis=0, concat_axis=0, tiled=True)
 
 
 def total_of(parts):
@@ -415,7 +422,7 @@
     own_partial = contract(own_ladder, flat_amplitudes, width)
     own_parts = spread(own_partial)
     other_partial = contract(other_ladder, flat_amplitudes, width)
-    other_parts = spread(other_partial)
+    other_parts = spread_twice(other_partial)
     sums = [
         total_of(parts).reshape(width, 2, parts.shape[2]) for parts in (own_parts, other_parts)
     ]

time: 320 us -> 360 us (1.12)
  waiting for transfers between devices: 151 us -> 180 us
  local copies, waits for them, and re-layouts: 20.4 us -> 26.2 us
  starting transfers between devices: 41.5 us -> 45.8 us
    ppermute x22, waiting for transfers between devices: 63.4 us -> 88.7 us  [flip(): return lax.ppermute(piece, axis, pairs)]
    all_to_all x0 -> x2, waiting for transfers between devices: none -> 7.58 us  [the longest x1 7.58 us: spread_twice(): return lax.all_to_all(plane, 'dev', split_axis=0, concat_axis=0, tiled=True)]
    all_to_all x0 -> x2, starting transfers between devices: none -> 7.14 us  [the longest x1 3.74 us: spread_twice(): lax.all_to_all(partial, 'col', split_axis=0, concat_axis=0, tiled=True)]
    unnamed x33 -> x35, local copies, waits for them, and re-layouts: 1.42 us -> 7.16 us
    all_to_all x2 -> x1, waiting for transfers between devices: 30.2 us -> 26.3 us  [spread(): lax.all_to_all(partial, ('col', 'dev'), split_axis=0, concat_axis=0, tile...]
    all_to_all x2 -> x1, starting transfers between devices: 7.53 us -> 4.68 us  [spread(): lax.all_to_all(partial, ('col', 'dev'), split_axis=0, concat_axis=0, tile...]
  transfers between devices with their start and end apart: 36 -> 37, of which waited for: 17 -> 18; matrix products, arithmetic and copies ran while one was open for 6% -> 6% of each run, Pallas kernels for 20% -> 11%
where the time goes in v1:
time: 360 us; the launch traced here: 359 us
  waiting for transfers between devices  180 us (50%)
  Pallas kernels  96.7 us (27%)
  starting transfers between devices  45.8 us (13%)
  local copies, waits for them, and re-layouts  26.2 us (7%)
  other arithmetic  9.49 us (3%)
    ppermute x22, waiting for transfers between devices, flip(): return lax.ppermute(piece, axis, pairs)  88.7 us
    pallas_call x2, Pallas kernels, contract(): pl.pallas_call(contract_kernel, grid=(depth // step,), in_specs=[pl.Block...  49.7 us
    ppermute x6, waiting for transfers between devices, on_ring(): return lax.ppermute(piece, axis, pairs)  28.1 us
    all_to_all x1, waiting for transfers between devices, spread(): lax.all_to_all(partial, ('col', 'dev'), split_axis=0, concat_axis=0, tile...  26.3 us
    pallas_call x1, Pallas kernels, ladder_of(): pl.pallas_call(ladder_kernel, grid=(c_block // step,), in_specs=[pl.Block...  24.8 us
    ppermute x3, waiting for transfers between devices, whole_metric(): shares.append(lax.ppermute(shares[0], 'dev', pairs))  20.3 us
    ppermute x22, starting transfers between devices, flip(): return lax.ppermute(piece, axis, pairs)  18.2 us
    transpose x8, local copies, waits for them, and re-layouts, plan_on_device(): left_pieces.append(jnp.transpose(here[h], (2, 0, 1)))  14.8 us
  transfers between devices with their start and end apart: 37, of which 18 were waited for; matrix products, arithmetic and copies ran while one was open for 6% of the time, Pallas kernels for 11%

profile of v1, /device:TPU:0, one launch (start us, length us, event | category | flops | bytes accessed | tf_op | source)
XLA Modules:
  0.0 359.1 jit_solution(87045552995181976)
XLA Ops:
  0.0 3.8 %constant_dynamic-slice_fusion = bf16[256,16,1,128]{3,2,1,0:T(2,128)(2,1)S(1)} fusion(bf16[256,16,2,128]{3,2,1,0:T(2,128)(2,1)} %bitcast.30, s32[]{:T(128)S(6)} %select_n.109), kind=kLoop, calls=%fused_computation.38 | loop fusion | bytes 2097156 | tf_op jit(solution)/shard_map/jit(dynamic_index_in_dim)/dynamic_slice | solution.py:388
  4.6 3.1 collective-permute-start.11
  7.7 1.6 collective-permute-start.10
  9.3 13.3 %collective-permute-done.11 = bf16[16,128,128]{2,1,0:T(8,128)(2,1)} collective-permute-done((bf16[16,128,128]{2,1,0:T(8,128)(2,1)S(1)}, bf16[16,128,128]{2,1,0:T(8,128)(2,1)}, u32[]{:S(2)}, u32[]{:S(2)}) %collective-permute-start.11) | collective-permute-done | bytes 524320 | tf_op jit(solution)/shard_map/ppermute | solution.py:72
  22.6 11.2 %collective-permute-done.10 = bf16[16,128,128]{2,1,0:T(8,128)(2,1)} collective-permute-done((bf16[16,128,128]{2,1,0:T(8,128)(2,1)S(1)}, bf16[16,128,128]{2,1,0:T(8,128)(2,1)}, u32[]{:S(2)}, u32[]{:S(2)}) %collective-permute-start.10) | collective-permute-done | bytes 524320 | tf_op jit(solution)/shard_map/ppermute | solution.py:72
  33.8 1.6 collective-permute-start
  35.5 2.8 collective-permute-start.1
  39.4 18.3 %collective-permute-done = bf16[32,1024]{1,0:T(8,128)(2,1)S(1)} collective-permute-done((bf16[32,1024]{1,0:T(8,128)(2,1)S(1)}, bf16[32,1024]{1,0:T(8,128)(2,1)S(1)}, u32[]{:S(2)}, u32[]{:S(2)}) %collective-permute-start) | collective-permute-done | bytes 65568 | tf_op jit(solution)/shard_map/ppermute | solution.py:109
  57.7 2.0 collective-permute-done.1
  59.7 1.6 collective-permute-start.3
  61.3 1.5 collective-permute-start.4
  63.3 5.7 %collective-permute-done.3.refs_1_ = bf16[128,1024]{1,0:T(8,128)(2,1)S(1)} collective-permute-done((bf16[128,1024]{1,0:T(8,128)(2,1)S(1)}, bf16[128,1024]{1,0:T(8,128)(2,1)S(1)}, u32[]{:S(2)}, u32[]{:S(2)}) %collective-permute-start.3) | collective-permute-done | bytes 262176 | tf_op jit(solution)/shard_map/ppermute | solution.py:112
  69.0 1.9 collective-permute-start.14
  71.0 3.8 %collective-permute-done.4.refs_2_ = bf16[128,1024]{1,0:T(8,128)(2,1)S(1)} collective-permute-done((bf16[128,1024]{1,0:T(8,128)(2,1)S(1)}, bf16[128,1024]{1,0:T(8,128)(2,1)S(1)}, u32[]{:S(2)}, u32[]{:S(2)}) %collective-permute-start.4) | collective-permute-done | bytes 262176 | tf_op jit(solution)/shard_map/ppermute | solution.py:112
  78.4 2.2 copy.20.refs_2_
  80.6 2.2 copy.21.refs_3_
  83.6 3.9 %shard_map.73 = (bf16[1024,1024]{1,0:T(8,128)(2,1)}, bf16[1024,1024]{1,0:T(8,128)(2,1)}) custom-call(s32[2]{0:T(128)} %pad_add_fusion.1.place_ref, bf16[128,1024]{1,0:T(8,128)(2,1)} %copy-done.6, bf16[128,1024]{1,0:T(8,128)(2,1)} %copy-done.7, bf16[128,1024]{1,0:T(8,128)(2,1)} %copy-done.8, bf16[128,1024]{1,0:T(8,128)(2,1)} %copy-done.9, ...), custom_call_target="tpu_custom_call" | custom-call | tf_op jit(solution)/shard_map/pallas_call | solution.py:116
  87.5 2.2 copy.22.refs_4_
  89.7 2.2 copy.23.refs_5_
  93.1 3.6 collective-permute-done.15
  96.7 2.2 copy.25.refs_7_
  98.9 8.7 %shard_map.74.own_ref = bf16[128,16,1024]{2,1,0:T(8,128)(2,1)} custom-call(bf16[1024,1024]{1,0:T(8,128)(2,1)} %get-tuple-element.20.metric_ref, bf16[128,16,128]{2,1,0:T(8,128)(2,1)} %copy.18.refs_0_, bf16[128,16,128]{2,1,0:T(8,128)(2,1)} %copy.19.refs_1_, bf16[128,16,128]{2,1,0:T(8,128)(2,1)} %copy.20.refs_2_, bf16[128,16,128]{2,1,0:T(8,128)(2,1)} %copy.21.refs_3_, ...), custom_call_target="tpu_custom_call" | custom-call | flops 4294967296 | bytes 10485760 | tf_op jit(solution)/shard_map/pallas_call | solution.py:140
  107.7 1.6 collective-permute-start.18
  109.3 1.5 collective-permute-start.17
  111.8 10.7 %collective-permute-done.18 = bf16[16,128,128]{2,1,0:T(8,128)(2,1)S(1)} collective-permute-done((bf16[16,128,128]{2,1,0:T(8,128)(2,1)S(1)}, bf16[16,128,128]{2,1,0:T(8,128)(2,1)S(1)}, u32[]{:S(2)}, u32[]{:S(2)}) %collective-permute-start.18) | collective-permute-done | bytes 524320 | tf_op jit(solution)/shard_map/ppermute | solution.py:77
  124.7 1.5 collective-permute-start.26
  126.2 7.6 %collective-permute-done.22 = bf16[16,128,128]{2,1,0:T(8,128)(2,1)S(1)} collective-permute-done((bf16[16,128,128]{2,1,0:T(8,128)(2,1)}, bf16[16,128,128]{2,1,0:T(8,128)(2,1)S(1)}, u32[]{:S(2)}, u32[]{:S(2)}) %collective-permute-start.22) | collective-permute-done | bytes 524320 | tf_op jit(solution)/shard_map/ppermute | solution.py:77
  138.1 17.6 %collective-permute-done.26 = bf16[16,128,128]{2,1,0:T(8,128)(2,1)S(1)} collective-permute-done((bf16[16,128,128]{2,1,0:T(8,128)(2,1)}, bf16[16,128,128]{2,1,0:T(8,128)(2,1)S(1)}, u32[]{:S(2)}, u32[]{:S(2)}) %collective-permute-start.26) | collective-permute-done | bytes 524320 | tf_op jit(solution)/shard_map/ppermute | solution.py:77
  155.7 1.5 collective-permute-start.30
  157.2 1.5 collective-permute-start.29
  161.3 9.4 %collective-permute-done.30 = bf16[16,128,128]{2,1,0:T(8,128)(2,1)S(1)} collective-permute-done((bf16[16,128,128]{2,1,0:T(8,128)(2,1)}, bf16[16,128,128]{2,1,0:T(8,128)(2,1)S(1)}, u32[]{:S(2)}, u32[]{:S(2)}) %collective-permute-start.30) | collective-permute-done | bytes 524320 | tf_op jit(solution)/shard_map/ppermute | solution.py:77
  170.7 1.5 collective-permute-start.27
  172.2 1.5 collective-permute-start.28
  174.9 7.1 %collective-permute-done.23.refs_5_ = bf16[16,128,128]{2,1,0:T(8,128)(2,1)S(1)} collective-permute-done((bf16[16,128,128]{2,1,0:T(8,128)(2,1)S(1)}, bf16[16,128,128]{2,1,0:T(8,128)(2,1)S(1)}, u32[]{:S(2)}, u32[]{:S(2)}) %collective-permute-start.23) | collective-permute-done | bytes 524320 | tf_op jit(solution)/shard_map/ppermute | solution.py:77
  181.9 1.5 collective-permute-start.31
  183.5 1.5 collective-permute-start.32
  185.0 8.1 %collective-permute-done.27.refs_9_ = bf16[16,128,128]{2,1,0:T(8,128)(2,1)S(1)} collective-permute-done((bf16[16,128,128]{2,1,0:T(8,128)(2,1)S(1)}, bf16[16,128,128]{2,1,0:T(8,128)(2,1)S(1)}, u32[]{:S(2)}, u32[]{:S(2)}) %collective-permute-start.27) | collective-permute-done | bytes 524320 | tf_op jit(solution)/shard_map/ppermute | solution.py:77
  194.5 9.7 %shard_map.75.early_ref = f32[1024,2048]{1,0:T(8,128)S(1)} custom-call(s32[2]{0:T(128)S(1)} %pad_add_fusion.arrived_ref, bf16[1024,1024]{1,0:T(8,128)(2,1)S(1)} %copy-done.2, bf16[16,128,128]{2,1,0:T(8,128)(2,1)S(1)} %broadcast_select_fusion.7.refs_0_, bf16[16,128,128]{2,1,0:T(8,128)(2,1)S(1)} %collective-permute-done.19.refs_1_, ...), custom_call_target="tpu_custom_call" | custom-call | flops 3221225472 | bytes 13107200 | tf_op jit(solution)/shard_map/pallas_call | solution.py:205
  204.2 24.8 %shard_map.76.ladder_ref = bf16[512,16384]{1,0:T(8,128)(2,1)} custom-call(s32[2]{0:T(128)S(1)} %pad_add_fusion.arrived_ref, bf16[1024,1024]{1,0:T(8,128)(2,1)S(1)} %copy-done.2, bf16[128,16,1024]{2,1,0:T(8,128)(2,1)S(1)} %copy-done.3, bf16[128,16,1024]{2,1,0:T(8,128)(2,1)} %collective-permute-done.16.other_ref, f32[1024,2048]{1,0:T(8,128)S(1)} %shard_map.75.early_ref, ...), custom_call_target="tpu_custom_call" | custom-call | flops 18253611008 | bytes 33554432 | tf_op jit(solution)/shard_map/pallas_call | solution.py:297
  229.1 25.4 %collective-permute-done.33.ladder_ref = bf16[512,16384]{1,0:T(8,128)(2,1)S(1)} collective-permute-done((bf16[512,16384]{1,0:T(8,128)(2,1)}, bf16[512,16384]{1,0:T(8,128)(2,1)S(1)}, u32[]{:S(2)}, u32[]{:S(2)}) %collective-permute-start.33) | collective-permute-done | bytes 16777248 | tf_op jit(solution)/shard_map/ppermute | solution.py:77
  254.4 5.7 %copy-done.16 = bf16[512,16384]{1,0:T(8,128)(2,1)} copy-done((bf16[512,16384]{1,0:T(8,128)(2,1)}, bf16[512,16384]{1,0:T(8,128)(2,1)S(1)}, u32[]{:S(2)}) %copy-start.16) | copy-done | bytes 16777240
  260.2 24.8 %shard_map.78 = bf16[16,32,1024]{2,1,0:T(8,128)(2,1)} custom-call(bf16[512,16384]{1,0:T(8,128)(2,1)} %copy-done.16, bf16[16384,1024]{1,0:T(8,128)(2,1)} %bitcast.34), custom_call_target="tpu_custom_call" | custom-call | flops 17179869184 | bytes 51380224 | tf_op jit(solution)/shard_map/pallas_call | solution.py:349
  285.0 3.7 %all-to-all-start.1 = ((bf16[16,32,1024]{2,1,0:T(8,128)(2,1)}), bf16[16,32,1024]{2,1,0:T(8,128)(2,1)S(1)}, u32[]{:S(2)}, u32[]{:S(2)}) async-start(bf16[16,32,1024]{2,1,0:T(8,128)(2,1)} %shard_map.78), calls=%async_computation.1 | async-start | bytes 2097152 | tf_op jit(solution)/shard_map/all_to_all | solution.py:374
  288.7 24.9 %shard_map.77 = bf16[16,32,1024]{2,1,0:T(8,128)(2,1)} custom-call(bf16[512,16384]{1,0:T(8,128)(2,1)} %shard_map.76.ladder_ref, bf16[16384,1024]{1,0:T(8,128)(2,1)} %bitcast.35), custom_call_target="tpu_custom_call" | custom-call | flops 17179869184 | bytes 51380224 | tf_op jit(solution)/shard_map/pallas_call | solution.py:349
  313.6 4.7 %all-to-all-start = ((bf16[16,32,1024]{2,1,0:T(8,128)(2,1)}), bf16[16,32,1024]{2,1,0:T(8,128)(2,1)S(1)}, u32[]{:S(2)}, u32[]{:S(2)}) async-start(bf16[16,32,1024]{2,1,0:T(8,128)(2,1)} %shard_map.77), calls=%async_computation | async-start | bytes 2097152 | tf_op jit(solution)/shard_map/all_to_all | solution.py:369
  319.5 26.3 %all-to-all-done = bf16[16,32,1024]{2,1,0:T(8,128)(2,1)S(1)} async-done(((bf16[16,32,1024]{2,1,0:T(8,128)(2,1)}), bf16[16,32,1024]{2,1,0:T(8,128)(2,1)S(1)}, u32[]{:S(2)}, u32[]{:S(2)}) %all-to-all-start) | async-done | bytes 1048608 | tf_op jit(solution)/shard_map/all_to_all | solution.py:369
  345.8 3.4 all-to-all-start.2
  349.8 7.6 %all-to-all-done.2 = bf16[4,32,1024]{2,1,0:T(8,128)(2,1)S(1)} async-done(((bf16[4,32,1024]{2,1,0:T(8,128)(2,1)}), bf16[4,32,1024]{2,1,0:T(8,128)(2,1)S(1)}, u32[]{:S(2)}, u32[]{:S(2)}) %all-to-all-start.2) | async-done | bytes 262176 | tf_op jit(solution)/shard_map/all_to_all | solution.py:376
  (106 shorter events, 24.0 us)
Async XLA Ops:
  0.0 33.8 %copy-start = (bf16[256,1024]{1,0:T(8,128)(2,1)S(1)}, bf16[256,1024]{1,0:T(8,128)(2,1)}, u32[]{:S(2)}) copy-start(bf16[256,1024]{1,0:T(8,128)(2,1)} %param.8) | copy-start | bytes 1572868
  4.6 18.0 %collective-permute-start.11 = (bf16[16,128,128]{2,1,0:T(8,128)(2,1)S(1)}, bf16[16,128,128]{2,1,0:T(8,128)(2,1)}, u32[]{:S(2)}, u32[]{:S(2)}) collective-permute-start(bf16[16,128,128]{2,1,0:T(8,128)(2,1)S(1)} %get-tuple-element.22), channel_id=1, source_target_pairs={{0,2},{2,4},{4,6},{6,0},{1,3},{3,5},{5,7},{7,1},{8,10},{10,12},{12... | collective-permute-start | bytes 1572872 | tf_op jit(solution)/shard_map/ppermute | solution.py:72
  7.7 26.1 %collective-permute-start.10 = (bf16[16,128,128]{2,1,0:T(8,128)(2,1)S(1)}, bf16[16,128,128]{2,1,0:T(8,128)(2,1)}, u32[]{:S(2)}, u32[]{:S(2)}) collective-permute-start(bf16[16,128,128]{2,1,0:T(8,128)(2,1)S(1)} %get-tuple-element.21), channel_id=1, source_target_pairs={{0,2},{2,4},{4,6},{6,0},{1,3},{3,5},{5,7},{7,1},{8,10},{10,12},{12... | collective-permute-start | bytes 1572872 | tf_op jit(solution)/shard_map/ppermute | solution.py:72
  22.6 48.3 %collective-permute-start.13 = (bf16[16,128,128]{2,1,0:T(8,128)(2,1)}, bf16[16,128,128]{2,1,0:T(8,128)(2,1)}, u32[]{:S(2)}, u32[]{:S(2)}) collective-permute-start(bf16[16,128,128]{2,1,0:T(8,128)(2,1)} %collective-permute-done.11), channel_id=1, source_target_pairs={{0,2},{2,4},{4,6},{6,0},{1,3},{3,5},{5,7},{7,1},{8,10},{10,12},{12... | collective-permute-start | bytes 1572872 | tf_op jit(solution)/shard_map/ppermute | solution.py:72
  33.8 35.2 %collective-permute-start.12 = (bf16[16,128,128]{2,1,0:T(8,128)(2,1)}, bf16[16,128,128]{2,1,0:T(8,128)(2,1)}, u32[]{:S(2)}, u32[]{:S(2)}) collective-permute-start(bf16[16,128,128]{2,1,0:T(8,128)(2,1)} %collective-permute-done.10), channel_id=1, source_target_pairs={{0,2},{2,4},{4,6},{6,0},{1,3},{3,5},{5,7},{7,1},{8,10},{10,12},{12... | collective-permute-start | bytes 1572872 | tf_op jit(solution)/shard_map/ppermute | solution.py:72
  33.8 23.8 %collective-permute-start = (bf16[32,1024]{1,0:T(8,128)(2,1)S(1)}, bf16[32,1024]{1,0:T(8,128)(2,1)S(1)}, u32[]{:S(2)}, u32[]{:S(2)}) collective-permute-start(bf16[32,1024]{1,0:T(8,128)(2,1)S(1)} %constant_dynamic-slice_fusion.1), channel_id=1, source_target_pairs={{0,2},{2,4},{4,6},{6,0},{1,3},{3,5},{5,7},{7,1},{8,10},{10,12},{12... | collective-permute-start | bytes 196616 | tf_op jit(solution)/shard_map/ppermute | solution.py:109
  35.5 24.2 %collective-permute-start.1 = (bf16[32,1024]{1,0:T(8,128)(2,1)S(1)}, bf16[32,1024]{1,0:T(8,128)(2,1)S(1)}, u32[]{:S(2)}, u32[]{:S(2)}) collective-permute-start(bf16[32,1024]{1,0:T(8,128)(2,1)S(1)} %constant_dynamic-slice_fusion.1), channel_id=1, source_target_pairs={{0,4},{2,6},{4,0},{6,2},{1,5},{3,7},{5,1},{7,3},{8,12},{10,14},{12... | collective-permute-start | bytes 196616 | tf_op jit(solution)/shard_map/ppermute | solution.py:109
  38.3 21.4 %collective-permute-start.2 = (bf16[32,1024]{1,0:T(8,128)(2,1)S(1)}, bf16[32,1024]{1,0:T(8,128)(2,1)S(1)}, u32[]{:S(2)}, u32[]{:S(2)}) collective-permute-start(bf16[32,1024]{1,0:T(8,128)(2,1)S(1)} %constant_dynamic-slice_fusion.1), channel_id=1, source_target_pairs={{0,6},{2,0},{4,2},{6,4},{1,7},{3,1},{5,3},{7,5},{8,14},{10,8},{12,... | collective-permute-start | bytes 196616 | tf_op jit(solution)/shard_map/ppermute | solution.py:109
  59.7 23.1 %copy-start.6 = (bf16[128,1024]{1,0:T(8,128)(2,1)}, bf16[128,1024]{1,0:T(8,128)(2,1)S(1)}, u32[]{:S(2)}) copy-start(bf16[128,1024]{1,0:T(8,128)(2,1)S(1)} %pad_maximum_fusion.refs_0_) | copy-start | bytes 786436
  59.7 9.2 %collective-permute-start.3 = (bf16[128,1024]{1,0:T(8,128)(2,1)S(1)}, bf16[128,1024]{1,0:T(8,128)(2,1)S(1)}, u32[]{:S(2)}, u32[]{:S(2)}) collective-permute-start(bf16[128,1024]{1,0:T(8,128)(2,1)S(1)} %pad_maximum_fusion.refs_0_), channel_id=1, source_target_pairs={{0,8},{8,0},{16,24},{24,16},{1,9},{9,1},{17,25},{25,17},{2,10},{10... | collective-permute-start | bytes 786440 | tf_op jit(solution)/shard_map/ppermute | solution.py:112
  61.3 13.5 %collective-permute-start.4 = (bf16[128,1024]{1,0:T(8,128)(2,1)S(1)}, bf16[128,1024]{1,0:T(8,128)(2,1)S(1)}, u32[]{:S(2)}, u32[]{:S(2)}) collective-permute-start(bf16[128,1024]{1,0:T(8,128)(2,1)S(1)} %pad_maximum_fusion.refs_0_), channel_id=1, source_target_pairs={{0,16},{8,24},{16,0},{24,8},{1,17},{9,25},{17,1},{25,9},{2,18},{10... | collective-permute-start | bytes 786440 | tf_op jit(solution)/shard_map/ppermute | solution.py:112
  62.8 12.0 %collective-permute-start.5 = (bf16[128,1024]{1,0:T(8,128)(2,1)S(1)}, bf16[128,1024]{1,0:T(8,128)(2,1)S(1)}, u32[]{:S(2)}, u32[]{:S(2)}) collective-permute-start(bf16[128,1024]{1,0:T(8,128)(2,1)S(1)} %pad_maximum_fusion.refs_0_), channel_id=1, source_target_pairs={{0,24},{8,16},{16,8},{24,0},{1,25},{9,17},{17,9},{25,1},{2,26},{10... | collective-permute-start | bytes 786440 | tf_op jit(solution)/shard_map/ppermute | solution.py:112
  69.0 13.9 %copy-start.7 = (bf16[128,1024]{1,0:T(8,128)(2,1)}, bf16[128,1024]{1,0:T(8,128)(2,1)S(1)}, u32[]{:S(2)}) copy-start(bf16[128,1024]{1,0:T(8,128)(2,1)S(1)} %collective-permute-done.3.refs_1_) | copy-start | bytes 786436
  69.0 6.3 %collective-permute-start.6 = (bf16[128,1024]{1,0:T(8,128)(2,1)S(1)}, bf16[128,1024]{1,0:T(8,128)(2,1)S(1)}, u32[]{:S(2)}, u32[]{:S(2)}) collective-permute-start(bf16[128,1024]{1,0:T(8,128)(2,1)S(1)} %pad_maximum_fusion.refs_0_), channel_id=1, source_target_pairs={{0,1},{1,0},{2,3},{3,2},{4,5},{5,4},{6,7},{7,6},{8,9},{9,8},{10,11... | collective-permute-start | bytes 786440 | tf_op jit(solution)/shard_map/ppermute | solution.py:77
  69.0 22.9 %collective-permute-start.14 = (bf16[16,128,128]{2,1,0:T(8,128)(2,1)}, bf16[16,128,128]{2,1,0:T(8,128)(2,1)S(1)}, u32[]{:S(2)}, u32[]{:S(2)}) collective-permute-start(bf16[16,128,128]{2,1,0:T(8,128)(2,1)} %collective-permute-done.12), channel_id=1, source_target_pairs={{0,2},{2,4},{4,6},{6,0},{1,3},{3,5},{5,7},{7,1},{8,10},{10,12},{12... | collective-permute-start | bytes 1572872 | tf_op jit(solution)/shard_map/ppermute | solution.py:72
  70.9 25.8 %collective-permute-start.15 = (bf16[16,128,128]{2,1,0:T(8,128)(2,1)}, bf16[16,128,128]{2,1,0:T(8,128)(2,1)}, u32[]{:S(2)}, u32[]{:S(2)}) collective-permute-start(bf16[16,128,128]{2,1,0:T(8,128)(2,1)} %collective-permute-done.13), channel_id=1, source_target_pairs={{0,2},{2,4},{4,6},{6,0},{1,3},{3,5},{5,7},{7,1},{8,10},{10,12},{12... | collective-permute-start | bytes 1572872 | tf_op jit(solution)/shard_map/ppermute | solution.py:72
  74.8 8.1 %copy-start.8 = (bf16[128,1024]{1,0:T(8,128)(2,1)}, bf16[128,1024]{1,0:T(8,128)(2,1)S(1)}, u32[]{:S(2)}) copy-start(bf16[128,1024]{1,0:T(8,128)(2,1)S(1)} %collective-permute-done.4.refs_2_) | copy-start | bytes 786436
  74.8 8.1 %collective-permute-start.7 = (bf16[128,1024]{1,0:T(8,128)(2,1)S(1)}, bf16[128,1024]{1,0:T(8,128)(2,1)S(1)}, u32[]{:S(2)}, u32[]{:S(2)}) collective-permute-start(bf16[128,1024]{1,0:T(8,128)(2,1)S(1)} %collective-permute-done.3.refs_1_), channel_id=1, source_target_pairs={{0,1},{1,0},{2,3},{3,2},{4,5},{5,4},{6,7},{7,6},{8,9},{9,8},{10,11... | collective-permute-start | bytes 786440 | tf_op jit(solution)/shard_map/ppermute | solution.py:77
  74.8 8.1 %copy-start.9 = (bf16[128,1024]{1,0:T(8,128)(2,1)}, bf16[128,1024]{1,0:T(8,128)(2,1)S(1)}, u32[]{:S(2)}) copy-start(bf16[128,1024]{1,0:T(8,128)(2,1)S(1)} %collective-permute-done.5.refs_3_) | copy-start | bytes 786436
  74.8 8.1 %collective-permute-start.8 = (bf16[128,1024]{1,0:T(8,128)(2,1)S(1)}, bf16[128,1024]{1,0:T(8,128)(2,1)}, u32[]{:S(2)}, u32[]{:S(2)}) collective-permute-start(bf16[128,1024]{1,0:T(8,128)(2,1)S(1)} %collective-permute-done.4.refs_2_), channel_id=1, source_target_pairs={{0,1},{1,0},{2,3},{3,2},{4,5},{5,4},{6,7},{7,6},{8,9},{9,8},{10,11... | collective-permute-start | bytes 786440 | tf_op jit(solution)/shard_map/ppermute | solution.py:77
  75.3 8.3 %collective-permute-start.9 = (bf16[128,1024]{1,0:T(8,128)(2,1)S(1)}, bf16[128,1024]{1,0:T(8,128)(2,1)}, u32[]{:S(2)}, u32[]{:S(2)}) collective-permute-start(bf16[128,1024]{1,0:T(8,128)(2,1)S(1)} %collective-permute-done.5.refs_3_), channel_id=1, source_target_pairs={{0,1},{1,0},{2,3},{3,2},{4,5},{5,4},{6,7},{7,6},{8,9},{9,8},{10,11... | collective-permute-start | bytes 786440 | tf_op jit(solution)/shard_map/ppermute | solution.py:77
  91.9 15.7 %copy-start.4 = (bf16[16,128,128]{2,1,0:T(8,128)(2,1)}, bf16[16,128,128]{2,1,0:T(8,128)(2,1)S(1)}, u32[]{:S(2)}) copy-start(bf16[16,128,128]{2,1,0:T(8,128)(2,1)S(1)} %collective-permute-done.14) | copy-start | bytes 1572868
  107.6 96.6 %collective-permute-start.16 = (bf16[128,16,1024]{2,1,0:T(8,128)(2,1)}, bf16[128,16,1024]{2,1,0:T(8,128)(2,1)}, u32[]{:S(2)}, u32[]{:S(2)}) collective-permute-start(bf16[128,16,1024]{2,1,0:T(8,128)(2,1)} %shard_map.74.own_ref), channel_id=1, source_target_pairs={{0,1},{1,0},{2,3},{3,2},{4,5},{5,4},{6,7},{7,6},{8,9},{9,8},{10,11... | collective-permute-start | bytes 12582920 | tf_op jit(solution)/shard_map/ppermute | solution.py:77
  107.7 14.9 %collective-permute-start.18 = (bf16[16,128,128]{2,1,0:T(8,128)(2,1)S(1)}, bf16[16,128,128]{2,1,0:T(8,128)(2,1)S(1)}, u32[]{:S(2)}, u32[]{:S(2)}) collective-permute-start(bf16[16,128,128]{2,1,0:T(8,128)(2,1)S(1)} %get-tuple-element.22), channel_id=1, source_target_pairs={{0,16},{8,24},{16,0},{24,8},{1,17},{9,25},{17,1},{25,9},{2,18},{10... | collective-permute-start | bytes 1572872 | tf_op jit(solution)/shard_map/ppermute | solution.py:77
  109.3 14.8 %collective-permute-start.17 = (bf16[16,128,128]{2,1,0:T(8,128)(2,1)S(1)}, bf16[16,128,128]{2,1,0:T(8,128)(2,1)S(1)}, u32[]{:S(2)}, u32[]{:S(2)}) collective-permute-start(bf16[16,128,128]{2,1,0:T(8,128)(2,1)S(1)} %get-tuple-element.21), channel_id=1, source_target_pairs={{0,8},{8,0},{16,24},{24,16},{1,9},{9,1},{17,25},{25,17},{2,10},{10... | collective-permute-start | bytes 1572872 | tf_op jit(solution)/shard_map/ppermute | solution.py:77
  110.7 23.0 %collective-permute-start.22 = (bf16[16,128,128]{2,1,0:T(8,128)(2,1)}, bf16[16,128,128]{2,1,0:T(8,128)(2,1)S(1)}, u32[]{:S(2)}, u32[]{:S(2)}) collective-permute-start(bf16[16,128,128]{2,1,0:T(8,128)(2,1)} %collective-permute-done.11), channel_id=1, source_target_pairs={{0,16},{8,24},{16,0},{24,8},{1,17},{9,25},{17,1},{25,9},{2,18},{10... | collective-permute-start | bytes 1572872 | tf_op jit(solution)/shard_map/ppermute | solution.py:77
  111.3 25.1 %collective-permute-start.21 = (bf16[16,128,128]{2,1,0:T(8,128)(2,1)}, bf16[16,128,128]{2,1,0:T(8,128)(2,1)S(1)}, u32[]{:S(2)}, u32[]{:S(2)}) collective-permute-start(bf16[16,128,128]{2,1,0:T(8,128)(2,1)} %collective-permute-done.10), channel_id=1, source_target_pairs={{0,8},{8,0},{16,24},{24,16},{1,9},{9,1},{17,25},{25,17},{2,10},{10... | collective-permute-start | bytes 1572872 | tf_op jit(solution)/shard_map/ppermute | solution.py:77
  122.6 34.6 %copy-start.5 = (bf16[16,128,128]{2,1,0:T(8,128)(2,1)S(1)}, bf16[16,128,128]{2,1,0:T(8,128)(2,1)}, u32[]{:S(2)}) copy-start(bf16[16,128,128]{2,1,0:T(8,128)(2,1)} %copy-done.4) | copy-start | bytes 1572868
  124.1 37.0 %collective-permute-start.19 = (bf16[16,128,128]{2,1,0:T(8,128)(2,1)S(1)}, bf16[16,128,128]{2,1,0:T(8,128)(2,1)S(1)}, u32[]{:S(2)}, u32[]{:S(2)}) collective-permute-start(bf16[16,128,128]{2,1,0:T(8,128)(2,1)S(1)} %broadcast_select_fusion.7.refs_0_), channel_id=1, source_target_pairs={{0,16},{8,24},{16,0},{24,8},{1,17},{9,25},{17,1},{25,9},{2,18},{10... | collective-permute-start | bytes 1572872 | tf_op jit(solution)/shard_map/ppermute | solution.py:77
  124.7 31.0 %collective-permute-start.26 = (bf16[16,128,128]{2,1,0:T(8,128)(2,1)}, bf16[16,128,128]{2,1,0:T(8,128)(2,1)S(1)}, u32[]{:S(2)}, u32[]{:S(2)}) collective-permute-start(bf16[16,128,128]{2,1,0:T(8,128)(2,1)} %collective-permute-done.13), channel_id=1, source_target_pairs={{0,16},{8,24},{16,0},{24,8},{1,17},{9,25},{17,1},{25,9},{2,18},{10... | collective-permute-start | bytes 1572872 | tf_op jit(solution)/shard_map/ppermute | solution.py:77
  133.8 23.5 %collective-permute-start.25 = (bf16[16,128,128]{2,1,0:T(8,128)(2,1)}, bf16[16,128,128]{2,1,0:T(8,128)(2,1)S(1)}, u32[]{:S(2)}, u32[]{:S(2)}) collective-permute-start(bf16[16,128,128]{2,1,0:T(8,128)(2,1)} %collective-permute-done.12), channel_id=1, source_target_pairs={{0,8},{8,0},{16,24},{24,16},{1,9},{9,1},{17,25},{25,17},{2,10},{10... | collective-permute-start | bytes 1572872 | tf_op jit(solution)/shard_map/ppermute | solution.py:77
  136.4 24.8 %collective-permute-start.20 = (bf16[16,128,128]{2,1,0:T(8,128)(2,1)S(1)}, bf16[16,128,128]{2,1,0:T(8,128)(2,1)S(1)}, u32[]{:S(2)}, u32[]{:S(2)}) collective-permute-start(bf16[16,128,128]{2,1,0:T(8,128)(2,1)S(1)} %broadcast_select_fusion.3.refs_2_), channel_id=1, source_target_pairs={{0,8},{8,0},{16,24},{24,16},{1,9},{9,1},{17,25},{25,17},{2,10},{10... | collective-permute-start | bytes 1572872 | tf_op jit(solution)/shard_map/ppermute | solution.py:77
  155.7 15.0 %collective-permute-start.30 = (bf16[16,128,128]{2,1,0:T(8,128)(2,1)}, bf16[16,128,128]{2,1,0:T(8,128)(2,1)S(1)}, u32[]{:S(2)}, u32[]{:S(2)}) collective-permute-start(bf16[16,128,128]{2,1,0:T(8,128)(2,1)} %collective-permute-done.15), channel_id=1, source_target_pairs={{0,16},{8,24},{16,0},{24,8},{1,17},{9,25},{17,1},{25,9},{2,18},{10... | collective-permute-start | bytes 1572872 | tf_op jit(solution)/shard_map/ppermute | solution.py:77
  157.2 15.0 %collective-permute-start.29 = (bf16[16,128,128]{2,1,0:T(8,128)(2,1)S(1)}, bf16[16,128,128]{2,1,0:T(8,128)(2,1)S(1)}, u32[]{:S(2)}, u32[]{:S(2)}) collective-permute-start(bf16[16,128,128]{2,1,0:T(8,128)(2,1)S(1)} %copy-done.5), channel_id=1, source_target_pairs={{0,8},{8,0},{16,24},{24,16},{1,9},{9,1},{17,25},{25,17},{2,10},{10... | collective-permute-start | bytes 1572872 | tf_op jit(solution)/shard_map/ppermute | solution.py:77
  159.8 34.7 %copy-start.2 = (bf16[1024,1024]{1,0:T(8,128)(2,1)S(1)}, bf16[1024,1024]{1,0:T(8,128)(2,1)}, u32[]{:S(2)}) copy-start(bf16[1024,1024]{1,0:T(8,128)(2,1)} %get-tuple-element.19.metric_ref) | copy-start | bytes 6291460
  161.1 20.8 %collective-permute-start.23 = (bf16[16,128,128]{2,1,0:T(8,128)(2,1)S(1)}, bf16[16,128,128]{2,1,0:T(8,128)(2,1)S(1)}, u32[]{:S(2)}, u32[]{:S(2)}) collective-permute-start(bf16[16,128,128]{2,1,0:T(8,128)(2,1)S(1)} %broadcast_select_fusion.6.refs_4_), channel_id=1, source_target_pairs={{0,16},{8,24},{16,0},{24,8},{1,17},{9,25},{17,1},{25,9},{2,18},{10... | collective-permute-start | bytes 1572872 | tf_op jit(solution)/shard_map/ppermute | solution.py:77
  161.2 22.3 %collective-permute-start.24 = (bf16[16,128,128]{2,1,0:T(8,128)(2,1)S(1)}, bf16[16,128,128]{2,1,0:T(8,128)(2,1)S(1)}, u32[]{:S(2)}, u32[]{:S(2)}) collective-permute-start(bf16[16,128,128]{2,1,0:T(8,128)(2,1)S(1)} %broadcast_select_fusion.2.refs_6_), channel_id=1, source_target_pairs={{0,8},{8,0},{16,24},{24,16},{1,9},{9,1},{17,25},{25,17},{2,10},{10... | collective-permute-start | bytes 1572872 | tf_op jit(solution)/shard_map/ppermute | solution.py:77
  170.7 22.5 %collective-permute-start.27 = (bf16[16,128,128]{2,1,0:T(8,128)(2,1)S(1)}, bf16[16,128,128]{2,1,0:T(8,128)(2,1)S(1)}, u32[]{:S(2)}, u32[]{:S(2)}) collective-permute-start(bf16[16,128,128]{2,1,0:T(8,128)(2,1)S(1)} %broadcast_select_fusion.5.refs_8_), channel_id=1, source_target_pairs={{0,16},{8,24},{16,0},{24,8},{1,17},{9,25},{17,1},{25,9},{2,18},{10... | collective-permute-start | bytes 1572872 | tf_op jit(solution)/shard_map/ppermute | solution.py:77
  172.2 22.3 %collective-permute-start.28 = (bf16[16,128,128]{2,1,0:T(8,128)(2,1)S(1)}, bf16[16,128,128]{2,1,0:T(8,128)(2,1)S(1)}, u32[]{:S(2)}, u32[]{:S(2)}) collective-permute-start(bf16[16,128,128]{2,1,0:T(8,128)(2,1)S(1)} %broadcast_select_fusion.1.refs_10_), channel_id=1, source_target_pairs={{0,8},{8,0},{16,24},{24,16},{1,9},{9,1},{17,25},{25,17},{2,10},{10... | collective-permute-start | bytes 1572872 | tf_op jit(solution)/shard_map/ppermute | solution.py:77
  181.9 22.2 %collective-permute-start.31 = (bf16[16,128,128]{2,1,0:T(8,128)(2,1)S(1)}, bf16[16,128,128]{2,1,0:T(8,128)(2,1)S(1)}, u32[]{:S(2)}, u32[]{:S(2)}) collective-permute-start(bf16[16,128,128]{2,1,0:T(8,128)(2,1)S(1)} %broadcast_select_fusion.4.refs_0_), channel_id=1, source_target_pairs={{0,16},{8,24},{16,0},{24,8},{1,17},{9,25},{17,1},{25,9},{2,18},{10... | collective-permute-start | bytes 1572872 | tf_op jit(solution)/shard_map/ppermute | solution.py:77
  183.5 20.7 %collective-permute-start.32 = (bf16[16,128,128]{2,1,0:T(8,128)(2,1)S(1)}, bf16[16,128,128]{2,1,0:T(8,128)(2,1)S(1)}, u32[]{:S(2)}, u32[]{:S(2)}) collective-permute-start(bf16[16,128,128]{2,1,0:T(8,128)(2,1)S(1)} %broadcast_select_fusion.refs_2_), channel_id=1, source_target_pairs={{0,8},{8,0},{16,24},{24,16},{1,9},{9,1},{17,25},{25,17},{2,10},{10... | collective-permute-start | bytes 1572872 | tf_op jit(solution)/shard_map/ppermute | solution.py:77
  194.5 9.7 %copy-start.3 = (bf16[128,16,1024]{2,1,0:T(8,128)(2,1)S(1)}, bf16[128,16,1024]{2,1,0:T(8,128)(2,1)}, u32[]{:S(2)}) copy-start(bf16[128,16,1024]{2,1,0:T(8,128)(2,1)} %shard_map.74.own_ref) | copy-start | bytes 12582916
  229.0 25.4 %collective-permute-start.33 = (bf16[512,16384]{1,0:T(8,128)(2,1)}, bf16[512,16384]{1,0:T(8,128)(2,1)S(1)}, u32[]{:S(2)}, u32[]{:S(2)}) collective-permute-start(bf16[512,16384]{1,0:T(8,128)(2,1)} %shard_map.76.ladder_ref), channel_id=1, source_target_pairs={{0,1},{1,0},{2,3},{3,2},{4,5},{5,4},{6,7},{7,6},{8,9},{9,8},{10,11... | collective-permute-start | bytes 50331656 | tf_op jit(solution)/shard_map/ppermute | solution.py:77
  285.0 28.6 %all-to-all-start.1 = ((bf16[16,32,1024]{2,1,0:T(8,128)(2,1)}), bf16[16,32,1024]{2,1,0:T(8,128)(2,1)S(1)}, u32[]{:S(2)}, u32[]{:S(2)}) async-start(bf16[16,32,1024]{2,1,0:T(8,128)(2,1)} %shard_map.78), calls=%async_computation.1 | async-start | bytes 2097152 | tf_op jit(solution)/shard_map/all_to_all | solution.py:374
  313.6 35.7 %copy-start.14 = (f32[64]{0:T(128)S(1)}, f32[64]{0:T(128)}, u32[]{:S(2)}) copy-start(f32[64]{0:T(128)} %param.11) | copy-start | bytes 772
  313.6 32.2 %all-to-all-start = ((bf16[16,32,1024]{2,1,0:T(8,128)(2,1)}), bf16[16,32,1024]{2,1,0:T(8,128)(2,1)S(1)}, u32[]{:S(2)}, u32[]{:S(2)}) async-start(bf16[16,32,1024]{2,1,0:T(8,128)(2,1)} %shard_map.77), calls=%async_computation | async-start | bytes 2097152 | tf_op jit(solution)/shard_map/all_to_all | solution.py:369
  345.8 11.6 %all-to-all-start.2 = ((bf16[4,32,1024]{2,1,0:T(8,128)(2,1)}), bf16[4,32,1024]{2,1,0:T(8,128)(2,1)S(1)}, u32[]{:S(2)}, u32[]{:S(2)}) async-start(bf16[4,32,1024]{2,1,0:T(8,128)(2,1)} %reduce_sum.76), calls=%async_computation.2 | async-start | bytes 524288 | tf_op jit(solution)/shard_map/all_to_all | solution.py:376
  349.5 9.6 %copy-start.1 = (bf16[256,1024]{1,0:T(8,128)(2,1)S(1)}, bf16[256,1024]{1,0:T(8,128)(2,1)}, u32[]{:S(2)}) copy-start(bf16[256,1024]{1,0:T(8,128)(2,1)} %param.8) | copy-start | bytes 1572868
  (6 other events, 28.5 us)
